TPU v7x, 32 devices: a whole 2x2x4 slice. The times are simulated.
32 devices in a mesh: dp: 16 (over z, x, core), ffn: 2 (over y).
Axes of the slice: x: 2, y: 2, z: 4, core: 2. Of those that a mesh axis runs over, the one named last changes fastest.
Arguments:
- inputs: bfloat16 [65536, 768], P(('dp', 'ffn')), may hold values from -6 to 6
- segments: int32 [128, 512], P(('dp', 'ffn')), may hold values from 0 to 3, never falling along the last dimension, each value on 1 to 256 neighbouring positions
- cotangent: bfloat16 [65536, 768], P(('dp', 'ffn')), may hold values from -6 to 6
- qkv_weight: bfloat16 [3, 4, 192, 192], replicated, may hold values from -0.4375 to 0.4375
- qv_bias: float32 [2, 768], replicated, may hold values from -1.75 to 1.75
- out_weight: bfloat16 [768, 768], replicated, may hold values from -2.5 to 2.5
- out_bias: float32 [768], replicated, may hold values from -1.75 to 1.75
- ln1_gain: float32 [768], replicated, may hold values from 0.1 to 1.9
- ln1_bias: float32 [768], replicated, may hold values from -1.75 to 1.75
- up_weight: bfloat16 [4, 192, 768], P(None, None, 'ffn'), may hold values from -0.4375 to 0.4375
- up_bias: bfloat16 [4, 768], P(None, 'ffn'), may hold values from -1.75 to 1.75
- down_weight: bfloat16 [4, 192, 768], P(None, None, 'ffn'), may hold values from -0.4375 to 0.4375
- down_bias: float32 [768], replicated, may hold values from -1.75 to 1.75
- ln2_gain: float32 [768], replicated, may hold values from 0.1 to 1.9
- ln2_bias: float32 [768], replicated, may hold values from -1.75 to 1.75
Outputs:
- layer_out: float32 [65536, 768], P(('dp', 'ffn'))
- grad_inputs: float32 [65536, 768], P(('dp', 'ffn'))
- grad_qkv_weight: float32 [3, 4, 192, 192], replicated
- grad_qv_bias: float32 [2, 768], replicated
- grad_out_weight: float32 [768, 768], replicated
- grad_out_bias: float32 [768], replicated
- grad_ln1_gain: float32 [768], replicated
- grad_ln1_bias: float32 [768], replicated
- grad_up_weight: float32 [4, 192, 768], P(None, None, 'ffn')
- grad_up_bias: float32 [4, 768], P(None, 'ffn')
- grad_down_weight: float32 [4, 192, 768], P(None, None, 'ffn')
- grad_down_bias: float32 [768], replicated
- grad_ln2_gain: float32 [768], replicated
- grad_ln2_bias: float32 [768], replicated
Inputs may be any that keep to these rules, and one draw needn't show every extreme that they name: `segments`: within each row the numbers never fall, start at 0 and count up by one; a document spans 1 to 256 positions.
All inputs are finite; a program needn't handle non-finite values.
Results may differ from a plain program's by a relative error of at most 0.013.
The roundings to bfloat16 on the way count: a program that leaves them out, or rounds other values in their place, can miss the bound.
Values may be sent and summed in bfloat16 or wider, within the bound.
No kernel may reach another device: no remote copies, remote signals or barrier semaphores. Data moves between devices by JAX's collectives and lax.ppermute only.
A program may use at most 256 MiB of HBM per device.

v0:
```python
from functools import partial

import jax
import jax.numpy as jnp
from jax import lax
from jax.sharding import PartitionSpec as P

HEADS = 12
HEAD_DIM = 64


norm_eps = 1e-05


def layer_norm(values, gain, shift):
    average = jnp.mean(values, axis=-1, keepdims=True)
    centered = values - average
    variance = jnp.mean(centered * centered, axis=-1, keepdims=True)
    inverse = lax.rsqrt(variance + norm_eps)
    normal = centered * inverse
    return (normal * gain + shift, normal, inverse)


def norm_back(grad_out, normal, inverse, gain):
    scaled = grad_out * gain
    inner = (
        scaled
        - jnp.mean(scaled, axis=-1, keepdims=True)
        - normal * jnp.mean(scaled * normal, axis=-1, keepdims=True)
    )
    return (inverse * inner, jnp.sum(grad_out * normal, axis=0), jnp.sum(grad_out, axis=0))


def grouped_in(values, weight):
    tok_count = values.shape[0]
    grouped = values.reshape(tok_count, weight.shape[0], weight.shape[1])
    return jnp.einsum("ngi,gio->ngo", grouped, weight, preferred_element_type=jnp.float32).reshape(
        tok_count, -1
    )


def grouped_out(values, weight):
    tok_count = values.shape[0]
    grouped = values.reshape(tok_count, weight.shape[0], weight.shape[2])
    return jnp.einsum("ngi,goi->ngo", grouped, weight, preferred_element_type=jnp.float32).reshape(
        tok_count, -1
    )


def back_in(gradient, weight):
    tok_count = gradient.shape[0]
    grouped = gradient.reshape(tok_count, weight.shape[0], weight.shape[2])
    return jnp.einsum("ngo,gio->ngi", grouped, weight, preferred_element_type=jnp.float32).reshape(
        tok_count, -1
    )


def back_out(gradient, weight):
    tok_count = gradient.shape[0]
    grouped = gradient.reshape(tok_count, weight.shape[0], weight.shape[1])
    return jnp.einsum("ngo,goi->ngi", grouped, weight, preferred_element_type=jnp.float32).reshape(
        tok_count, -1
    )


def weight_in(values, gradient, groups):
    tok_count = values.shape[0]
    return jnp.einsum(
        "ngi,ngo->gio",
        values.reshape(tok_count, groups, -1),
        gradient.reshape(tok_count, groups, -1),
        preferred_element_type=jnp.float32,
    )


def weight_out(values, gradient, groups):
    tok_count = values.shape[0]
    return jnp.einsum(
        "ngi,ngo->goi",
        values.reshape(tok_count, groups, -1),
        gradient.reshape(tok_count, groups, -1),
        preferred_element_type=jnp.float32,
    )


def row_scores(query, keyed, segment):
    seq_len = query.shape[0]
    head_q = query.reshape(seq_len, HEADS, HEAD_DIM)
    head_k = keyed.reshape(seq_len, HEADS, HEAD_DIM)
    raw_scores = jnp.einsum("qhd,khd->hqk", head_q, head_k, preferred_element_type=jnp.float32)
    same_doc = segment[:, None] == segment[None, :]
    scores = jnp.where(same_doc[None, :, :], raw_scores * HEAD_DIM ** (-0.5), -1e30)
    return (scores, head_q, head_k)


def row_forward(packed):
    query, keyed, valued, segment = packed
    scores, head_q, head_k = row_scores(query, keyed, segment)
    row_peak = jnp.max(scores, axis=-1, keepdims=True)
    exponent = jnp.exp(scores - row_peak)
    row_total = jnp.sum(exponent, axis=-1, keepdims=True)
    weights = (exponent / row_total).astype(jnp.bfloat16)
    head_v = valued.reshape(query.shape[0], HEADS, HEAD_DIM)
    mixed = jnp.einsum("hqk,khd->qhd", weights, head_v, preferred_element_type=jnp.float32)
    return (mixed.reshape(query.shape), row_peak + jnp.log(row_total))


def row_backward(packed):
    query, keyed, valued, segment, log_total, grad_mixed = packed
    scores, head_q, head_k = row_scores(query, keyed, segment)
    softmax_out = jnp.exp(scores - log_total)
    weights = softmax_out.astype(jnp.bfloat16)
    head_v = valued.reshape(query.shape[0], HEADS, HEAD_DIM)
    head_grad = grad_mixed.reshape(query.shape[0], HEADS, HEAD_DIM)
    grad_weights = jnp.einsum("qhd,khd->hqk", head_grad, head_v, preferred_element_type=jnp.float32)
    grad_value = jnp.einsum("hqk,qhd->khd", weights, head_grad, preferred_element_type=jnp.float32)
    row_delta = jnp.sum(grad_weights * softmax_out, axis=-1, keepdims=True)
    grad_scores = (softmax_out * (grad_weights - row_delta) * HEAD_DIM ** (-0.5)).astype(
        jnp.bfloat16
    )
    grad_query = jnp.einsum("hqk,khd->qhd", grad_scores, head_k, preferred_element_type=jnp.float32)
    grad_key = jnp.einsum("hqk,qhd->khd", grad_scores, head_q, preferred_element_type=jnp.float32)
    return (
        grad_query.reshape(query.shape),
        grad_key.reshape(query.shape),
        grad_value.reshape(query.shape),
    )


def per_device(
    inputs,
    segments,
    cotangent,
    qkv_weight,
    qv_bias,
    out_weight,
    out_bias,
    ln1_gain,
    ln1_bias,
    up_weight,
    up_bias,
    down_weight,
    down_bias,
    ln2_gain,
    ln2_bias,
):
    tok_count, model_width = inputs.shape
    row_count, seq_len = segments.shape
    groups = qkv_weight.shape[1]
    by_rows = (row_count, seq_len, model_width)
    query = (grouped_in(inputs, qkv_weight[0]) + qv_bias[0]).astype(jnp.bfloat16)
    keyed = grouped_in(inputs, qkv_weight[1]).astype(jnp.bfloat16)
    valued = (grouped_in(inputs, qkv_weight[2]) + qv_bias[1]).astype(jnp.bfloat16)
    row_query = query.reshape(by_rows)
    row_key = keyed.reshape(by_rows)
    row_value = valued.reshape(by_rows)
    attended, log_total = lax.map(row_forward, (row_query, row_key, row_value, segments))
    attended_low = attended.reshape(tok_count, model_width).astype(jnp.bfloat16)
    mixed = jnp.dot(attended_low, out_weight, preferred_element_type=jnp.float32) + out_bias
    normed, normal_one, inverse_one = layer_norm(
        inputs.astype(jnp.float32) + mixed, ln1_gain, ln1_bias
    )
    normed_low = normed.astype(jnp.bfloat16)
    gelu_exact = partial(jax.nn.gelu, approximate=False)
    ffn_input = lax.all_gather(normed_low, "ffn", axis=0, tiled=True)
    up_full, down_full, bias_full = (up_weight, down_weight, up_bias)
    upward = grouped_in(ffn_input, up_full) + bias_full.astype(jnp.float32).reshape(-1)
    activated_full, gelu_back = jax.vjp(gelu_exact, upward)
    activated = activated_full.astype(jnp.bfloat16)
    row_block = lax.slice_in_dim(activated, 0, lax.axis_size("ffn") * tok_count, axis=0)
    downward = lax.psum_scatter(
        grouped_out(row_block, down_full), "ffn", scatter_dimension=0, tiled=True
    )
    layer_out, normal_two, inverse_two = layer_norm(
        normed + downward + down_bias, ln2_gain, ln2_bias
    )
    grad_sum_two, grad_ln2_gain, grad_ln2_bias = norm_back(
        cotangent.astype(jnp.float32), normal_two, inverse_two, ln2_gain
    )
    grad_down_bias = jnp.sum(grad_sum_two, axis=0)
    grad_down_low = grad_sum_two.astype(jnp.bfloat16)
    grad_ffn_out = lax.all_gather(grad_down_low, "ffn", axis=0, tiled=True)
    grad_activated = back_out(grad_ffn_out, down_full)
    grad_down_weight = weight_out(activated, grad_ffn_out, groups)
    grad_upward = gelu_back(grad_activated)[0]
    grad_up_bias = jnp.sum(grad_upward, axis=0).reshape(up_full.shape[0], up_full.shape[2])
    grad_up_low = grad_upward.astype(jnp.bfloat16)
    grad_up_weight = weight_in(ffn_input, grad_up_low, groups)
    row_block = grad_up_low
    grad_normed_ffn = lax.psum_scatter(
        back_in(row_block, up_full), "ffn", scatter_dimension=0, tiled=True
    )
    grad_normed = grad_sum_two + grad_normed_ffn
    grad_sum_one, grad_ln1_gain, grad_ln1_bias = norm_back(
        grad_normed, normal_one, inverse_one, ln1_gain
    )
    grad_out_bias = jnp.sum(grad_sum_one, axis=0)
    grad_mixed_low = grad_sum_one.astype(jnp.bfloat16)
    grad_out_weight = jnp.einsum(
        "nd,ne->de", attended_low, grad_mixed_low, preferred_element_type=jnp.float32
    )
    grad_attended = jnp.einsum(
        "ne,de->nd", grad_mixed_low, out_weight, preferred_element_type=jnp.float32
    ).astype(jnp.bfloat16)
    grad_query, grad_key, grad_value = lax.map(
        row_backward,
        (row_query, row_key, row_value, segments, log_total, grad_attended.reshape(by_rows)),
    )
    grad_query = grad_query.reshape(tok_count, model_width)
    grad_key = grad_key.reshape(tok_count, model_width)
    grad_value = grad_value.reshape(tok_count, model_width)
    grad_qv_bias = jnp.stack([jnp.sum(grad_query, axis=0), jnp.sum(grad_value, axis=0)])
    grad_lows = [grad_part.astype(jnp.bfloat16) for grad_part in (grad_query, grad_key, grad_value)]
    grad_qkv_weight = jnp.stack([weight_in(inputs, grad_part, groups) for grad_part in grad_lows])
    grad_inputs = (
        grad_sum_one
        + back_in(grad_lows[0], qkv_weight[0])
        + back_in(grad_lows[1], qkv_weight[1])
        + back_in(grad_lows[2], qkv_weight[2])
    )
    shared = lax.psum(
        (
            grad_qkv_weight,
            grad_qv_bias,
            grad_out_weight,
            grad_out_bias,
            grad_ln1_gain,
            grad_ln1_bias,
            grad_down_bias,
            grad_ln2_gain,
            grad_ln2_bias,
        ),
        ("dp", "ffn"),
    )
    ffn_sums = lax.psum((grad_up_weight, grad_up_bias, grad_down_weight), "dp")
    return (
        layer_out,
        grad_inputs,
        shared[0],
        shared[1],
        shared[2],
        shared[3],
        shared[4],
        shared[5],
        ffn_sums[0],
        ffn_sums[1],
        ffn_sums[2],
        shared[6],
        shared[7],
        shared[8],
    )


def solution(mesh):
    in_specs = (
        P(("dp", "ffn"), None),
        P(("dp", "ffn"), None),
        P(("dp", "ffn"), None),
        P(),
        P(),
        P(),
        P(),
        P(),
        P(),
        P(None, None, "ffn"),
        P(None, "ffn"),
        P(None, None, "ffn"),
        P(),
        P(),
        P(),
    )
    out_specs = (
        P(("dp", "ffn"), None),
        P(("dp", "ffn"), None),
        P(),
        P(),
        P(),
        P(),
        P(),
        P(),
        P(None, None, "ffn"),
        P(None, "ffn"),
        P(None, None, "ffn"),
        P(),
        P(),
        P(),
    )
    return jax.shard_map(
        per_device, mesh=mesh, in_specs=in_specs, out_specs=out_specs, check_vma=False
    )
```

profile of v0, /device:TPU:1, one launch (start us, length us, event | category | flops | bytes accessed | tf_op | source)
XLA Modules:
  0.0 1333.8 jit_solution(11613991013185107814)
XLA Ops:
  51.6 12.2 fusion.75
  63.8 55.2 %while.26 = (s32[]{:T(128)}, bf16[4,512,768]{2,1,0:T(8,128)(2,1)}, f32[4,12,512,1]{2,1,3,0:T(8,128)}, bf16[4,512,768]{1,2,0:T(8,128)(2,1)}, s32[4,512]{1,0:T(4,1...) while((s32[]{:T(128)}, bf16[4,512,768]{2,1,0:T(8,128)(2,1)}, ...), condition=%wide.region_3.4_spmd, body=%wide.region_0.3_spmd.sunk | while | flops 843311104 | bytes 50019424 | solution.py:157
  131.2 82.5 %all-gather.3.cloned.1.call-done = bf16[4096,768]{0,1:T(8,128)(2,1)} async-done(((bf16[2048,768]{0,1:T(8,128)(2,1)}), bf16[4096,768]{0,1:T(8,128)(2,1)}) %all-gather.3.cloned.1.call-update) | async-done | bytes 6291472 | tf_op jit(solution)/shard_map/all_gather | solution.py:165
  213.8 61.0 %fusion.55 = (bf16[4096,4,384]{2,0,1:T(8,128)(2,1)S(1)}, f32[4096,4,384]{2,0,1:T(8,128)}, f32[4,4096,384]{2,1,0:T(8,128)}) fusion(f32[4,384]{1,0:T(4,128)S(1)} %convert_element_type.92, bf16[4096,4,192]{0,2,1:T(8,128)(2,1)} %bitcast.291, bf16[4,192,384]{2,1,0:T(8,128)(2,1)S(1)} %copy-done.19), kind=kOutput, calls=%fused_computation.67 | convolution fusion | flops 2831155200 | bytes 69801984 | tf_op jit(solution)/shard_map/ngi,gio->ngo/dot_general | solution.py:37
  287.9 139.8 %reduce-scatter.3.cloned.1.call-done = f32[2048,768]{0,1:T(8,128)} async-done(((f32[4096,768]{0,1:T(8,128)}), f32[2048,768]{0,1:T(8,128)}) %reduce-scatter.3.cloned.1.call-update) | async-done | bytes 6291472 | tf_op jit(solution)/shard_map/reduce_scatter | solution.py:171
  443.1 80.5 %all-gather.5.cloned.1.call-done = bf16[4096,768]{0,1:T(8,128)(2,1)} async-done(((bf16[2048,768]{0,1:T(8,128)(2,1)}), bf16[4096,768]{0,1:T(8,128)(2,1)}) %all-gather.5.cloned.1.call-update) | async-done | bytes 6291472 | tf_op jit(solution)/shard_map/all_gather | solution.py:182
  523.6 28.1 %fusion.111 = (f32[4,384]{1,0:T(4,128)}, bf16[4096,4,384]{2,0,1:T(8,128)(2,1)}) fusion(f32[4096,4,384]{2,0,1:T(8,128)} %get-tuple-element.235, bf16[4096,4,192]{0,2,1:T(8,128)(2,1)} %bitcast.293, bf16[4,192,384]{2,1,0:T(8,128)(2,1)S(1)} %copy-done.18, f32[4,4096,384]{2,1,0:T(8,128)} %get-tuple-element.254, f32[4,384]{1,0:T(4,128)S(1)} %convert_element_type.92), kind=kOutput, calls=%fused_computation.161 | convolution fusion | flops 2516580864 | bytes 69808128 | tf_op jit(solution)/shard_map/ngo,goi->ngi/dot_general | solution.py:61
  561.9 144.5 %reduce-scatter.5.cloned.1.call-done = f32[2048,768]{0,1:T(8,128)} async-done(((f32[4096,768]{0,1:T(8,128)}), f32[2048,768]{0,1:T(8,128)}) %reduce-scatter.5.cloned.1.call-update) | async-done | bytes 6291472 | tf_op jit(solution)/shard_map/reduce_scatter | solution.py:190
  706.4 14.1 %fusion.74 = (f32[768]{0:T(1024)}, f32[768]{0:T(1024)}, f32[768]{0:T(1024)}, f32[768]{0:T(1024)}, f32[2048]{0:T(1024)S(1)}, /*index=5*/f32[2048]{0:T(1024)S(1)},...) fusion(bf16[2048,768]{0,1:T(8,128)(2,1)} %copy.68, f32[2048,768]{0,1:T(8,128)} %copy-done.1, ...), kind=kLoop, calls=%fused_computation.90 | loop fusion | flops 37740800 | bytes 34693120 | tf_op jit(solution)/shard_map/reduce_sum | solution.py:31
  733.6 289.1 %while.27 = (s32[]{:T(128)}, f32[4,512,768]{1,2,0:T(8,128)}, bf16[4,512,768]{1,2,0:T(8,128)(2,1)}, f32[4,512,768]{1,2,0:T(8,128)}, bf16[4,512,768]{1,2,0:T(8,128...) while((s32[]{:T(128)}, f32[4,512,768]{1,2,0:T(8,128)}, ...), condition=%wide.region_16.17_spmd, body=%wide.region_14.16_spmd.sunk | while | flops 2095330304 | bytes 120814776 | solution.py:205
  756.8 20.4 %fusion.194 = f32[12,64,512]{2,1,0:T(8,128)} fusion(bf16[512,12,64]{0,2,1:T(8,128)(2,1)S(1)} %bitcast.280, f32[12,512,512]{1,2,0:T(8,128)} %fusion.193, f32[12,512,512]{1,2,0:T(8,128)} %fusion.191, f32[12,512]{1,0:T(8,128)} %dynamic-slice_bitcast_fusion.2, pred[512,512]{0,1:T(8,128)(4,1)} %broadcast_compare_fusion.5), kind=kOutput, calls=%fused_computation.22.clone.1 | convolution fusion | flops 437262848 | bytes 27811840 | tf_op jit(solution)/shard_map/while/body/eval_jaxpr/hqk,khd->qhd/dot_general | solution.py:121
  785.5 19.7 %fusion.195 = bf16[12,64,512]{2,1,0:T(8,128)(2,1)S(1)} fusion(bf16[512,12,64]{0,2,1:T(8,128)(2,1)S(1)} %bitcast.278, f32[12,512,512]{1,2,0:T(8,128)} %fusion.193, f32[12,512,512]{1,2,0:T(8,128)} %fusion.191, f32[12,512]{1,0:T(8,128)S(1)} %copy-done.17, pred[512,512]{0,1:T(8,128)(4,1)} %broadcast_compare_fusion.5), kind=kOutput, calls=%fused_computation.21.clone.1 | convolution fusion | flops 437262848 | bytes 27025408 | tf_op jit(solution)/shard_map/while/body/eval_jaxpr/hqk,qhd->khd/dot_general | solution.py:122
  828.9 20.4 %fusion.194 = f32[12,64,512]{2,1,0:T(8,128)} fusion(bf16[512,12,64]{0,2,1:T(8,128)(2,1)S(1)} %bitcast.280, f32[12,512,512]{1,2,0:T(8,128)} %fusion.193, f32[12,512,512]{1,2,0:T(8,128)} %fusion.191, f32[12,512]{1,0:T(8,128)} %dynamic-slice_bitcast_fusion.2, pred[512,512]{0,1:T(8,128)(4,1)} %broadcast_compare_fusion.5), kind=kOutput, calls=%fused_computation.22.clone.1 | convolution fusion | flops 437262848 | bytes 27811840 | tf_op jit(solution)/shard_map/while/body/eval_jaxpr/hqk,khd->qhd/dot_general | solution.py:121
  857.6 19.7 %fusion.195 = bf16[12,64,512]{2,1,0:T(8,128)(2,1)S(1)} fusion(bf16[512,12,64]{0,2,1:T(8,128)(2,1)S(1)} %bitcast.278, f32[12,512,512]{1,2,0:T(8,128)} %fusion.193, f32[12,512,512]{1,2,0:T(8,128)} %fusion.191, f32[12,512]{1,0:T(8,128)S(1)} %copy-done.17, pred[512,512]{0,1:T(8,128)(4,1)} %broadcast_compare_fusion.5), kind=kOutput, calls=%fused_computation.21.clone.1 | convolution fusion | flops 437262848 | bytes 27025408 | tf_op jit(solution)/shard_map/while/body/eval_jaxpr/hqk,qhd->khd/dot_general | solution.py:122
  901.0 20.4 %fusion.194 = f32[12,64,512]{2,1,0:T(8,128)} fusion(bf16[512,12,64]{0,2,1:T(8,128)(2,1)S(1)} %bitcast.280, f32[12,512,512]{1,2,0:T(8,128)} %fusion.193, f32[12,512,512]{1,2,0:T(8,128)} %fusion.191, f32[12,512]{1,0:T(8,128)} %dynamic-slice_bitcast_fusion.2, pred[512,512]{0,1:T(8,128)(4,1)} %broadcast_compare_fusion.5), kind=kOutput, calls=%fused_computation.22.clone.1 | convolution fusion | flops 437262848 | bytes 27811840 | tf_op jit(solution)/shard_map/while/body/eval_jaxpr/hqk,khd->qhd/dot_general | solution.py:121
  929.7 19.7 %fusion.195 = bf16[12,64,512]{2,1,0:T(8,128)(2,1)S(1)} fusion(bf16[512,12,64]{0,2,1:T(8,128)(2,1)S(1)} %bitcast.278, f32[12,512,512]{1,2,0:T(8,128)} %fusion.193, f32[12,512,512]{1,2,0:T(8,128)} %fusion.191, f32[12,512]{1,0:T(8,128)S(1)} %copy-done.17, pred[512,512]{0,1:T(8,128)(4,1)} %broadcast_compare_fusion.5), kind=kOutput, calls=%fused_computation.21.clone.1 | convolution fusion | flops 437262848 | bytes 27025408 | tf_op jit(solution)/shard_map/while/body/eval_jaxpr/hqk,qhd->khd/dot_general | solution.py:122
  973.2 20.4 %fusion.194 = f32[12,64,512]{2,1,0:T(8,128)} fusion(bf16[512,12,64]{0,2,1:T(8,128)(2,1)S(1)} %bitcast.280, f32[12,512,512]{1,2,0:T(8,128)} %fusion.193, f32[12,512,512]{1,2,0:T(8,128)} %fusion.191, f32[12,512]{1,0:T(8,128)} %dynamic-slice_bitcast_fusion.2, pred[512,512]{0,1:T(8,128)(4,1)} %broadcast_compare_fusion.5), kind=kOutput, calls=%fused_computation.22.clone.1 | convolution fusion | flops 437262848 | bytes 27811840 | tf_op jit(solution)/shard_map/while/body/eval_jaxpr/hqk,khd->qhd/dot_general | solution.py:121
  1001.9 19.7 %fusion.195 = bf16[12,64,512]{2,1,0:T(8,128)(2,1)S(1)} fusion(bf16[512,12,64]{0,2,1:T(8,128)(2,1)S(1)} %bitcast.278, f32[12,512,512]{1,2,0:T(8,128)} %fusion.193, f32[12,512,512]{1,2,0:T(8,128)} %fusion.191, f32[12,512]{1,0:T(8,128)S(1)} %copy-done.17, pred[512,512]{0,1:T(8,128)(4,1)} %broadcast_compare_fusion.5), kind=kOutput, calls=%fused_computation.21.clone.1 | convolution fusion | flops 437262848 | bytes 27025408 | tf_op jit(solution)/shard_map/while/body/eval_jaxpr/hqk,qhd->khd/dot_general | solution.py:122
  1075.0 11.2 fusion.115
  1086.2 31.5 %psum.91 = f32[4,384]{1,0:T(4,128)} all-reduce(f32[4,384]{1,0:T(4,128)S(1)} %copy-done.36), channel_id=1, replica_groups=mesh['dp'=16,'ffn'=2] {'dp'}, use_global_device_ids=true, to_apply=%region_30.31 | all-reduce | flops 1536 | bytes 12288 | tf_op jit(solution)/shard_map/psum | solution.py:235
  1117.7 11.1 fusion.77
  1141.9 14.5 %bitcast_add_fusion = f32[2048,768]{0,1:T(8,128)} fusion(f32[4,2048,192]{1,2,0:T(8,128)} %fusion.92, f32[4,2048,192]{1,2,0:T(8,128)} %fusion.86, f32[2048,768]{0,1:T(8,128)} %copy-done.7, f32[4,2048,192]{1,2,0:T(8,128)} %fusion.89), kind=kLoop, calls=%fused_computation.91 | loop fusion | flops 4718592 | bytes 31457280 | tf_op jit(solution)/shard_map/add | solution.py:216
  1169.7 41.7 %all-reduce = (f32[2,768]{1,0:T(2,128)}, f32[768]{0:T(1024)}, f32[768]{0:T(1024)}, f32[768]{0:T(1024)}, f32[768]{0:T(1024)}, /*index=5*/f32[768]{0:T(1024)}, f32[768]{0:T(1024)}) all-reduce(f32[2,768]{1,0:T(2,128)S(1)} %pad_maximum_fusion.1, f32[768]{0:T(1024)S(1)} %copy-done.32, ...), channel_id=1, replica_groups=mesh['dp'=16,'ffn'=2] {'dp','ffn'}, use_global_device_ids=true, to_apply=%region_20.21 | all-reduce | flops 6144 | bytes 49152 | tf_op jit(solution)/shard_map/psum | solution.py:221
  1222.3 99.5 %all-reduce.8.cloned.1.call-done = (f32[4,192,384]{2,1,0:T(8,128)}, f32[4,192,384]{2,1,0:T(8,128)}) async-done(((f32[4,192,384]{2,1,0:T(8,128)}, f32[4,192,384]{2,1,0:T(8,128)}), (f32[4,192,384]{2,1,0:T(8,128)}, f32[4,192,384]{2,1,0:T(8,128)})) %all-reduce.8.cloned.1.call-update) | async-done | bytes 2359312 | tf_op jit(solution)/shard_map/psum | solution.py:235
  (261 shorter events, 385.1 us)
Async XLA Ops:
  7.2 111.9 %copy-start = (bf16[768,768]{1,0:T(8,128)(2,1)S(1)}, bf16[768,768]{1,0:T(8,128)(2,1)}, u32[]{:S(2)}) copy-start(bf16[768,768]{1,0:T(8,128)(2,1)} %param.24) | copy-start | bytes 3538948
  7.2 206.6 %all-gather.3.cloned.1.call-start = ((), (), s32[]{:S(2)}) async-start(), calls=%async_computation.2 | async-start | bytes 9437184 | tf_op jit(solution)/shard_map/all_gather | solution.py:165
  32.9 8.4 copy-start.35
  63.8 55.2 %copy-start.41 = (f32[768]{0:T(1024)S(1)}, f32[768]{0:T(1024)}, u32[]{:S(2)}) copy-start(f32[768]{0:T(1024)} %param.25) | copy-start | bytes 9220
  128.5 85.3 %copy-start.19 = (bf16[4,192,384]{2,1,0:T(8,128)(2,1)S(1)}, bf16[4,192,384]{2,1,0:T(8,128)(2,1)}, u32[]{:S(2)}) copy-start(bf16[4,192,384]{2,1,0:T(8,128)(2,1)} %param.28) | copy-start | bytes 1769476
  131.2 296.6 %reduce-scatter.3.cloned.1.call-start = ((), (), s32[]{:S(2)}) async-start(), calls=%async_computation.3 | async-start | bytes 18874368 | tf_op jit(solution)/shard_map/reduce_scatter | solution.py:171
  213.8 61.0 %copy-start.18 = (bf16[4,192,384]{2,1,0:T(8,128)(2,1)S(1)}, bf16[4,192,384]{2,1,0:T(8,128)(2,1)}, u32[]{:S(2)}) copy-start(bf16[4,192,384]{2,1,0:T(8,128)(2,1)} %param.30) | copy-start | bytes 1769476
  274.8 8.3 copy-start.4
  283.1 144.6 %copy-start.21 = (f32[2048]{0:T(1024)S(1)}, f32[2048]{0:T(1024)}, u32[]{:S(2)}) copy-start(f32[2048]{0:T(1024)} %copy-done.20) | copy-start | bytes 24580
  283.1 144.6 %copy-start.23 = (f32[2048]{0:T(1024)S(1)}, f32[2048]{0:T(1024)}, u32[]{:S(2)}) copy-start(f32[2048]{0:T(1024)} %copy-done.22) | copy-start | bytes 24580
  283.1 144.6 %copy-start.25 = (f32[768]{0:T(1024)S(1)}, f32[768]{0:T(1024)}, u32[]{:S(2)}) copy-start(f32[768]{0:T(1024)} %param.26) | copy-start | bytes 9220
  283.1 144.6 %copy-start.34 = (f32[768]{0:T(1024)S(1)}, f32[768]{0:T(1024)}, u32[]{:S(2)}) copy-start(f32[768]{0:T(1024)} %param.27) | copy-start | bytes 9220
  283.2 144.6 %copy-start.38 = (f32[768]{0:T(1024)S(1)}, f32[768]{0:T(1024)}, u32[]{:S(2)}) copy-start(f32[768]{0:T(1024)} %param.31) | copy-start | bytes 9220
  283.2 240.4 %all-gather.5.cloned.1.call-start = ((), (), s32[]{:S(2)}) async-start(), calls=%async_computation.4 | async-start | bytes 9437184 | tf_op jit(solution)/shard_map/all_gather | solution.py:182
  443.0 263.4 %reduce-scatter.5.cloned.1.call-start = ((), (), s32[]{:S(2)}) async-start(), calls=%async_computation.5 | async-start | bytes 18874368 | tf_op jit(solution)/shard_map/reduce_scatter | solution.py:190
  561.8 144.6 %copy-start.37 = (f32[768]{0:T(1024)S(1)}, f32[768]{0:T(1024)}, u32[]{:S(2)}) copy-start(f32[768]{0:T(1024)} %param.33) | copy-start | bytes 9220
  561.8 657.1 %all-reduce.6.cloned.1.call-start = ((), (), s32[]{:S(2)}) async-start(), calls=%async_computation.6 | async-start | bytes 9437184 | tf_op jit(solution)/shard_map/psum | solution.py:221
  1022.8 7.3 copy-start.13
  1075.0 11.2 copy-start.36
  1075.0 246.8 %all-reduce.8.cloned.1.call-start = ((), (), s32[]{:S(2)}) async-start(), calls=%async_computation.7 | async-start | bytes 4718592 | tf_op jit(solution)/shard_map/psum | solution.py:235
  1117.7 11.1 copy-start.12
  1163.0 6.7 copy-start.31
  1163.0 6.7 copy-start.32
  1219.0 102.8 %copy-start.15 = (f32[768,768]{1,0:T(8,128)S(1)}, f32[768,768]{1,0:T(8,128)}, u32[]{:S(2)}) copy-start(f32[768,768]{1,0:T(8,128)} %get-tuple-element.438) | copy-start | bytes 7077892
  (30 other events, 130.3 us)
Sparse Core Ops, SparseCore 0:
  131.3 82.4 all-gather.2
  283.2 144.4 reduce-scatter.2
  443.2 80.3 all-gather.4
  561.9 144.4 reduce-scatter.4
  1075.1 143.8 all-reduce.5
  1223.4 98.3 all-reduce.7
where the time goes:
time: 1350 us; the launch traced here: 1330 us
  waiting for transfers between devices  554 us (41%)
  matrix products  440 us (33%)
  local copies, waits for them, and re-layouts  162 us (12%)
  other arithmetic  87.8 us (7%)
  blocking collectives  73.2 us (5%)
  between operations  14.9 us (1%)
    reduce_scatter x1, waiting for transfers between devices, per_device(): lax.psum_scatter(back_in(row_block, up_full), 'ffn', scatter_dimension=0,...  145 us
    reduce_scatter x1, waiting for transfers between devices, per_device(): lax.psum_scatter(grouped_out(row_block, down_full), 'ffn', scatter_dimens...  140 us
    psum x1, waiting for transfers between devices, per_device(): ffn_sums = lax.psum((grad_up_weight, grad_up_bias, grad_down_weight), 'dp')  99.5 us
    all_gather x1, waiting for transfers between devices, per_device(): ffn_input = lax.all_gather(normed_low, 'ffn', axis=0, tiled=True)  82.5 us
    dot_general x4, matrix products, row_backward(): jnp.einsum('hqk,khd->qhd', grad_scores, head_k, preferred_element_type=jn...  81.5 us
    all_gather x1, waiting for transfers between devices, per_device(): grad_ffn_out = lax.all_gather(grad_down_low, 'ffn', axis=0, tiled=True)  80.5 us
    dot_general x4, matrix products, row_backward(): jnp.einsum('hqk,qhd->khd', grad_scores, head_q, preferred_element_type=jn...  78.8 us
    dot_general x4, matrix products, grouped_in(): jnp.einsum('ngi,gio->ngo', grouped, weight, preferred_element_type=jnp.fl...  73.3 us
  transfers between devices with their start and end apart: 6, of which 6 were waited for; matrix products, arithmetic and copies ran while one was open for 5% of the time, Pallas kernels for 0%

commit v1 on v0

v1 whole, which is shorter than its diff:
```python
from functools import partial

import jax
import jax.numpy as jnp
from jax import lax
from jax.experimental import pallas as pl
from jax.experimental.pallas import tpu as pltpu
from jax.sharding import PartitionSpec as P

HEADS = 12
HEAD_DIM = 64
EPS = 1e-05
NEG = -1e30
VMEM = 60 * 1024 * 1024
BF = jnp.bfloat16
F32 = jnp.float32


def dot_nn(a, b):
    return jnp.dot(a, b, preferred_element_type=F32)


def dot_nt(a, b):
    return lax.dot_general(a, b, (((1,), (1,)), ((), ())), preferred_element_type=F32)


def params(*sem):
    return pltpu.CompilerParams(vmem_limit_bytes=VMEM, dimension_semantics=sem)


def wide(column, lanes):
    return jnp.concatenate([column] * (lanes // 128), axis=1)


def fold(values):
    total = values[:, 0:128]
    for start in range(128, values.shape[1], 128):
        total = total + values[:, start : start + 128]
    return total


def sub_sum(values):
    total = values[0:8]
    for start in range(8, values.shape[0], 8):
        total = total + values[start : start + 8]
    return total


def attend_kernel(x_ref, seg_ref, wt_ref, bias_ref, xt_ref, qkv_ref, att_ref, lse_ref, qa_ref, ka_ref):
    seq, width = x_ref.shape
    groups = wt_ref.shape[1]
    group = width // groups
    xt_ref[0] = x_ref[...].T
    seg = seg_ref[0]
    rank = lax.broadcasted_iota(jnp.int32, (16, seq), 0)
    same = rank == seg
    qa_ref[64:80, :] = jnp.where(same, 1.0, 0.0).astype(BF)
    ka_ref[64:80, :] = jnp.where(same | (rank >= 4), 0.0, NEG).astype(BF)

    def project(g, carry):
        rows = pl.ds(pl.multiple_of(g * group, group), group)
        xg = xt_ref[0, rows, :]
        for j in range(3):
            out = dot_nn(wt_ref[j, g], xg) + wide(bias_ref[j, rows, :], seq)
            qkv_ref[0, j, rows, :] = out.astype(BF)
        return carry

    lax.fori_loop(0, groups, project, 0)

    def head(h, carry):
        rows = pl.ds(pl.multiple_of(h * HEAD_DIM, HEAD_DIM), HEAD_DIM)
        qa_ref[0:64, :] = qkv_ref[0, 0, rows, :] * jnp.asarray(0.125, BF)
        ka_ref[0:64, :] = qkv_ref[0, 1, rows, :]
        kn = ka_ref[...].T
        vt = qkv_ref[0, 2, rows, :]
        for t in range(seq // 256):
            cols = slice(t * 256, t * 256 + 256)
            s = dot_nn(kn, qa_ref[:, cols])
            peak = jnp.max(s, axis=0, keepdims=True)
            e = jnp.exp(s - peak)
            total = jnp.sum(e, axis=0, keepdims=True)
            p = (e * (1.0 / total)).astype(BF)
            att_ref[0, rows, cols] = dot_nn(vt, p).astype(BF)
            lse_ref[0, pl.ds(h, 1), cols] = peak + jnp.log(total)
        return carry

    lax.fori_loop(0, HEADS, head, 0)


def attend(x, seg, wt, bias):
    width = x.shape[1]
    rows, seq = seg.shape
    return pl.pallas_call(
        attend_kernel,
        grid=(rows,),
        in_specs=[
            pl.BlockSpec((seq, width), lambda r: (r, 0)),
            pl.BlockSpec((1, 1, seq), lambda r: (r, 0, 0)),
            pl.BlockSpec(wt.shape, lambda r: (0, 0, 0, 0)),
            pl.BlockSpec(bias.shape, lambda r: (0, 0, 0)),
        ],
        out_specs=[
            pl.BlockSpec((1, width, seq), lambda r: (r, 0, 0)),
            pl.BlockSpec((1, 3, width, seq), lambda r: (r, 0, 0, 0)),
            pl.BlockSpec((1, width, seq), lambda r: (r, 0, 0)),
            pl.BlockSpec((1, 16, seq), lambda r: (r, 0, 0)),
        ],
        out_shape=[
            jax.ShapeDtypeStruct((rows, width, seq), BF),
            jax.ShapeDtypeStruct((rows, 3, width, seq), BF),
            jax.ShapeDtypeStruct((rows, width, seq), BF),
            jax.ShapeDtypeStruct((rows, 16, seq), F32),
        ],
        scratch_shapes=[pltpu.VMEM((80, seq), BF), pltpu.VMEM((80, seq), BF)],
        compiler_params=params("arbitrary"),
        name="attend",
    )(x, seg.reshape(rows, 1, seq), wt, bias)


CH = 128


def ffn_kernel(
    xt_ref, att_ref, cot_ref, wot_ref, wo_ref, wu_ref, wut_ref, wd_ref, wdt_ref, vec_ref,
    out_ref, gr1_ref, gatt_ref, delta_ref, dwo_ref, dff_ref, sums_ref,
    a_ref, u1_ref, v2_ref, nlow_ref, act_ref, gp_ref, gd_ref, gup_ref, ct_ref, acc_ref,
):
    width, seq = a_ref.shape
    halves, groups = wu_ref.shape[:2]
    group = width // groups
    part = wut_ref.shape[2]
    first = pl.program_id(0) == 0
    last = pl.program_id(0) == pl.num_programs(0) - 1
    inv_width = 1.0 / width

    @pl.when(first)
    def _():
        acc_ref[...] = jnp.zeros_like(acc_ref)
        dwo_ref[...] = jnp.zeros_like(dwo_ref)
        dff_ref[...] = jnp.zeros_like(dff_ref)
        row = lax.broadcasted_iota(jnp.int32, (16, seq), 0)
        for g in range(groups):
            nlow_ref[g, group : group + 16, :] = jnp.where(row == 0, 1.0, 0.0).astype(BF)

    ct_ref[...] = cot_ref[...].T

    part_sum = jnp.zeros((8, seq), F32)
    for c in range(0, width, CH):
        s = slice(c, c + CH)
        v = dot_nn(wot_ref[s, :], att_ref[0]) + wide(vec_ref[0, s, :], seq) + xt_ref[0, s, :].astype(F32)
        a_ref[s, :] = v
        part_sum = part_sum + sub_sum(v)
    mean = jnp.sum(part_sum, axis=0, keepdims=True) * inv_width
    part_sum = jnp.zeros((8, seq), F32)
    for c in range(0, width, CH):
        s = slice(c, c + CH)
        v = a_ref[s, :] - mean
        a_ref[s, :] = v
        part_sum = part_sum + sub_sum(v * v)
    r1 = lax.rsqrt(jnp.sum(part_sum, axis=0, keepdims=True) * inv_width + EPS)
    for g in range(groups):
        for c in range(0, group, 64):
            s = slice(g * group + c, g * group + c + 64)
            u = a_ref[s, :] * r1
            u1_ref[s, :] = u
            n = u * wide(vec_ref[1, s, :], seq) + wide(vec_ref[2, s, :], seq)
            v2_ref[s, :] = n + wide(vec_ref[3, s, :], seq)
            nlow_ref[g, c : c + 64, :] = n.astype(BF)

    def up(i, carry):
        h, g = i // groups, i % groups
        for c in range(0, part, CH):
            s = slice(c, c + CH)
            u = dot_nn(wut_ref[h, g, s, :], nlow_ref[g])
            y = u * 0.7071067811865476
            one = 1.0 + lax.erf(y)
            act_ref[i, s, :] = (u * one).astype(BF)
            gp_ref[i, s, :] = one + (y * 1.1283791670955126) * jnp.exp(-(y * y))
        rows = pl.ds(pl.multiple_of(g * group, group), group)
        v2_ref[rows, :] += dot_nn(wd_ref[h, g], act_ref[i])
        return carry

    lax.fori_loop(0, halves * groups, up, 0)

    part_sum = jnp.zeros((8, seq), F32)
    for c in range(0, width, CH):
        part_sum = part_sum + sub_sum(v2_ref[c : c + CH, :])
    mean = jnp.sum(part_sum, axis=0, keepdims=True) * inv_width
    part_sum = jnp.zeros((8, seq), F32)
    for c in range(0, width, CH):
        s = slice(c, c + CH)
        v = v2_ref[s, :] - mean
        v2_ref[s, :] = v
        part_sum = part_sum + sub_sum(v * v)
    r2 = lax.rsqrt(jnp.sum(part_sum, axis=0, keepdims=True) * inv_width + EPS)
    sum_e = jnp.zeros((8, seq), F32)
    sum_eu = jnp.zeros((8, seq), F32)
    for c in range(0, width, CH):
        s = slice(c, c + CH)
        u = v2_ref[s, :] * r2
        v2_ref[s, :] = u
        gain = wide(vec_ref[4, s, :], seq)
        out_ref[:, s] = (u * gain + wide(vec_ref[5, s, :], seq)).T
        cot = ct_ref[s, :].astype(F32)
        acc_ref[4, s, :] += fold(cot * u)
        acc_ref[5, s, :] += fold(cot)
        e = cot * gain
        sum_e = sum_e + sub_sum(e)
        sum_eu = sum_eu + sub_sum(e * u)
    mean_e = jnp.sum(sum_e, axis=0, keepdims=True) * inv_width
    mean_eu = jnp.sum(sum_eu, axis=0, keepdims=True) * inv_width
    for c in range(0, width, CH):
        s = slice(c, c + CH)
        e = ct_ref[s, :].astype(F32) * wide(vec_ref[4, s, :], seq)
        gr = r2 * (e - mean_e - v2_ref[s, :] * mean_eu)
        a_ref[s, :] = gr
        acc_ref[3, s, :] += fold(gr)
        gd_ref[s, :] = gr.astype(BF)

    def down(i, carry):
        h, g = i // groups, i % groups
        rows = pl.ds(pl.multiple_of(g * group, group), group)
        for c in range(0, part, CH):
            s = slice(c, c + CH)
            gup_ref[s, :] = (dot_nn(wdt_ref[h, g, s, :], gd_ref[rows, :]) * gp_ref[i, s, :]).astype(BF)
        dff_ref[h, g, 0 : group + 16, :] += dot_nt(nlow_ref[g], gup_ref[...])
        dff_ref[h, g, group + 16 : 2 * group + 16, :] += dot_nt(gd_ref[rows, :], act_ref[i])
        a_ref[rows, :] += dot_nn(wu_ref[h, g], gup_ref[...])
        return carry

    lax.fori_loop(0, halves * groups, down, 0)

    sum_e = jnp.zeros((8, seq), F32)
    sum_eu = jnp.zeros((8, seq), F32)
    for c in range(0, width, CH):
        s = slice(c, c + CH)
        gn = a_ref[s, :]
        u = u1_ref[s, :]
        acc_ref[1, s, :] += fold(gn * u)
        acc_ref[2, s, :] += fold(gn)
        e = gn * wide(vec_ref[1, s, :], seq)
        sum_e = sum_e + sub_sum(e)
        sum_eu = sum_eu + sub_sum(e * u)
    mean_e = jnp.sum(sum_e, axis=0, keepdims=True) * inv_width
    mean_eu = jnp.sum(sum_eu, axis=0, keepdims=True) * inv_width
    for c in range(0, width, CH):
        s = slice(c, c + CH)
        e = a_ref[s, :] * wide(vec_ref[1, s, :], seq)
        gr = r1 * (e - mean_e - u1_ref[s, :] * mean_eu)
        gr1_ref[0, s, :] = gr
        acc_ref[0, s, :] += fold(gr)
        gd_ref[s, :] = gr.astype(BF)
    for c in range(0, width, CH):
        s = slice(c, c + CH)
        ga = dot_nn(wo_ref[s, :], gd_ref[...]).astype(BF)
        gatt_ref[0, s, :] = ga
        prod = ga.astype(F32) * att_ref[0, s, :].astype(F32)
        for k in range(0, CH, HEAD_DIM):
            head = (c + k) // HEAD_DIM
            delta_ref[0, head : head + 1, :] = jnp.sum(prod[k : k + HEAD_DIM], axis=0, keepdims=True)
        dwo_ref[s, :] += dot_nt(att_ref[0, s, :], gd_ref[...])

    @pl.when(last)
    def _():
        dff_ref[:, :, group + 16 : 2 * group + 16, :] = dff_ref[:, :, group + 16 : 2 * group + 16, :] * 0.5
        for n in range(6):
            sums_ref[n : n + 1, :] = jnp.sum(acc_ref[n].T, axis=0, keepdims=True)
        sums_ref[6:8, :] = jnp.zeros((2, width), F32)


def feed(xt, att, cot, wot, wo, wu, wut, wd, wdt, vec):
    rows, width, seq = xt.shape
    halves, groups, group, part = wu.shape

    def whole(a):
        return pl.BlockSpec(a.shape, lambda r: (0,) * len(a.shape))

    per_row = pl.BlockSpec((1, width, seq), lambda r: (r, 0, 0))
    token = pl.BlockSpec((seq, width), lambda r: (r, 0))
    outs = [
        jax.ShapeDtypeStruct((rows * seq, width), F32),
        jax.ShapeDtypeStruct((rows, width, seq), F32),
        jax.ShapeDtypeStruct((rows, width, seq), BF),
        jax.ShapeDtypeStruct((rows, 16, seq), F32),
        jax.ShapeDtypeStruct((width, width), F32),
        jax.ShapeDtypeStruct((halves, groups, 2 * group + 32, part), F32),
        jax.ShapeDtypeStruct((8, width), F32),
    ]
    return pl.pallas_call(
        ffn_kernel,
        grid=(rows,),
        in_specs=[per_row, per_row, token] + [whole(a) for a in (wot, wo, wu, wut, wd, wdt, vec)],
        out_specs=[token, per_row, per_row, pl.BlockSpec((1, 16, seq), lambda r: (r, 0, 0))]
        + [whole(a) for a in outs[4:]],
        out_shape=outs,
        scratch_shapes=[
            pltpu.VMEM((width, seq), F32),
            pltpu.VMEM((width, seq), F32),
            pltpu.VMEM((width, seq), F32),
            pltpu.VMEM((groups, group + 16, seq), BF),
            pltpu.VMEM((halves * groups, part, seq), BF),
            pltpu.VMEM((halves * groups, part, seq), F32),
            pltpu.VMEM((width, seq), BF),
            pltpu.VMEM((part, seq), BF),
            pltpu.VMEM((width, seq), BF),
            pltpu.VMEM((6, width, 128), F32),
        ],
        compiler_params=params("arbitrary"),
        name="feed",
    )(xt, att, cot, wot, wo, wu, wut, wd, wdt, vec)


def split3(v):
    hi = v.astype(BF).astype(F32)
    mid = (v - hi).astype(BF).astype(F32)
    return hi, mid, v - hi - mid


def back_kernel(
    qkv_ref, gatt_ref, xt_ref, gr1_ref, lse_ref, delta_ref, seg_ref, w_ref, *rest, head0
):
    gin_ref, dw_ref, bsum_ref, qa_ref, ka_ref, va_ref, ga_ref, p_ref, ds_ref, d_ref = rest[-10:]
    chans, seq = xt_ref.shape[1:]
    groups, group = w_ref.shape[1:3]
    first = pl.program_id(0) == 0

    @pl.when(first)
    def _():
        dw_ref[...] = jnp.zeros_like(dw_ref)
        bsum_ref[...] = jnp.zeros_like(bsum_ref)

    seg = seg_ref[0]
    rank = lax.broadcasted_iota(jnp.int32, (16, seq), 0)
    same = rank == seg
    hot = jnp.where(same, 1.0, 0.0)
    ka_ref[64:80, :] = jnp.where(rank < 4, jnp.where(same, 0.0, NEG), jnp.where(rank < 7, -1.0, 0.0)).astype(BF)
    va_ref[64:80, :] = jnp.where(rank < 3, -1.0, 0.0).astype(BF)

    def head(h, carry):
        rows = pl.ds(pl.multiple_of(h * HEAD_DIM, HEAD_DIM), HEAD_DIM)
        hi, mid, lo = split3(lse_ref[0, pl.ds(head0 + h, 1), :])
        tail = jnp.where(rank == 4, hi, jnp.where(rank == 5, mid, jnp.where(rank == 6, lo, 0.0)))
        qa_ref[64:80, :] = jnp.where(rank < 4, hot, tail).astype(BF)
        hi, mid, lo = split3(delta_ref[0, pl.ds(head0 + h, 1), :])
        ga_ref[64:80, :] = jnp.where(rank == 0, hi, jnp.where(rank == 1, mid, jnp.where(rank == 2, lo, 0.0))).astype(BF)
        qs = qkv_ref[0, 0, rows, :] * jnp.asarray(0.125, BF)
        kt = qkv_ref[0, 1, rows, :]
        gt = gatt_ref[0, rows, :]
        qa_ref[0:64, :] = qs
        ka_ref[0:64, :] = kt
        va_ref[0:64, :] = qkv_ref[0, 2, rows, :]
        ga_ref[0:64, :] = gt
        kn = ka_ref[...].T
        vn = va_ref[...].T
        dk = jnp.zeros((HEAD_DIM, seq), F32)
        dv = jnp.zeros((HEAD_DIM, seq), F32)
        dq = []
        for t in range(seq // 256):
            cols = slice(t * 256, t * 256 + 256)
            p = jnp.exp(dot_nn(kn, qa_ref[:, cols]))
            p_ref[t] = p.astype(BF)
            ds_ref[t] = (p * dot_nn(vn, ga_ref[:, cols])).astype(BF)
            dv = dv + dot_nt(gt[:, cols], p_ref[t])
            dk = dk + dot_nt(qs[:, cols], ds_ref[t])
            dq.append(dot_nn(kt, ds_ref[t]) * 0.125)
        dq = jnp.concatenate(dq, axis=1)
        bsum_ref[0, rows, :] += fold(dq)
        bsum_ref[1, rows, :] += fold(dv)
        d_ref[0, rows, :] = dq.astype(BF)
        d_ref[1, rows, :] = dk.astype(BF)
        d_ref[2, rows, :] = dv.astype(BF)
        return carry

    lax.fori_loop(0, chans // HEAD_DIM, head, 0)
    parts = []
    for g in range(groups):
        s = slice(g * group, (g + 1) * group)
        total = gr1_ref[0, s, :]
        for j in range(3):
            d = d_ref[j, s, :]
            dw_ref[j, g] += dot_nt(xt_ref[0, s, :], d)
            total = total + dot_nn(w_ref[j, g], d)
        parts.append(total)
    gin_ref[...] = jnp.concatenate(parts, axis=0).T


def back(qkv, gatt, xt, gr1, lse, delta, seg, w, index, parts, into):
    rows, _, width, seq = qkv.shape
    chans = width // parts
    groups, group = w.shape[1] // parts, w.shape[2]
    per_row = pl.BlockSpec((1, chans, seq), lambda r: (r, index, 0))
    full = pl.BlockSpec((1, 16, seq), lambda r: (r, 0, 0))
    in_specs = [
        pl.BlockSpec((1, 3, chans, seq), lambda r: (r, 0, index, 0)),
        per_row,
        per_row,
        per_row,
        full,
        full,
        pl.BlockSpec((1, 1, seq), lambda r: (r, 0, 0)),
        pl.BlockSpec((3, groups, group, group), lambda r: (0, index, 0, 0)),
    ]
    args = [qkv, gatt, xt, gr1, lse, delta, seg.reshape(rows, 1, seq), w]
    alias = {}
    if into is not None:
        in_specs.append(pl.BlockSpec(memory_space=pl.ANY))
        args.append(into)
        alias = {len(args) - 1: 0}
    return pl.pallas_call(
        partial(back_kernel, head0=index * (chans // HEAD_DIM)),
        grid=(rows,),
        in_specs=in_specs,
        out_specs=[
            pl.BlockSpec((seq, chans), lambda r: (r, index)),
            pl.BlockSpec((3, groups, group, group), lambda r: (0, 0, 0, 0)),
            pl.BlockSpec((2, chans, 128), lambda r: (0, 0, 0)),
        ],
        out_shape=[
            jax.ShapeDtypeStruct((rows * seq, width), F32),
            jax.ShapeDtypeStruct((3, groups, group, group), F32),
            jax.ShapeDtypeStruct((2, chans, 128), F32),
        ],
        scratch_shapes=[pltpu.VMEM((80, seq), BF) for _ in range(4)]
        + [pltpu.VMEM((seq // 256, seq, 256), BF) for _ in range(2)]
        + [pltpu.VMEM((3, chans, seq), BF)],
        input_output_aliases=alias,
        compiler_params=params("arbitrary"),
        name="back",
    )(*args)


def swap(value, axis, size, bit):
    return lax.ppermute(value, axis, [(i, i ^ bit) for i in range(size)])


def scatter(value, axis, size, bit):
    half = value.shape[0] // 2
    mine = (lax.axis_index(axis) // bit) % 2
    keep = lax.dynamic_slice_in_dim(value, mine * half, half, 0)
    send = lax.dynamic_slice_in_dim(value, (1 - mine) * half, half, 0).astype(BF)
    return keep + swap(send, axis, size, bit).astype(F32)


def gather(value, axis, size, bit):
    mine = (lax.axis_index(axis) // bit) % 2
    other = swap(value, axis, size, bit)
    return jnp.where(mine == 0, jnp.concatenate([value, other]), jnp.concatenate([other, value]))


def sum_over(value, steps):
    done = []
    for axis, size, bit in steps:
        if value.shape[0] % 2 == 0:
            value = scatter(value, axis, size, bit)
            done.append((axis, size, bit))
        else:
            low = value.astype(BF)
            value = low.astype(F32) + swap(low, axis, size, bit).astype(F32)
    low = value.astype(BF)
    for step in reversed(done):
        low = gather(low, *step)
    return low.astype(F32)


def bits_of(axis, size):
    return [(axis, size, 1 << k) for k in range(size.bit_length() - 1)]


def per_device(
    inputs, segments, cotangent, qkv_weight, qv_bias, out_weight, out_bias, ln1_gain, ln1_bias,
    up_weight, up_bias, down_weight, down_bias, ln2_gain, ln2_bias, *, dp, ffn,
):
    width = inputs.shape[1]
    groups, group = qkv_weight.shape[1:3]
    part = up_weight.shape[2]

    def all_parts(a):
        return lax.all_gather(a, "ffn", axis=0)

    up_aug = jnp.concatenate(
        [up_weight, up_bias[:, None, :], jnp.zeros((groups, 15, part), BF)], axis=1
    )
    up_all = all_parts(up_aug)
    down_all = all_parts(down_weight)

    def lanes(v):
        return jnp.broadcast_to(v[..., None], v.shape + (128,))

    bias = lanes(jnp.stack([qv_bias[0], jnp.zeros_like(qv_bias[0]), qv_bias[1]]))
    xt, qkv, att, lse = attend(inputs, segments, qkv_weight.swapaxes(2, 3), bias)
    vec = lanes(jnp.stack([out_bias, ln1_gain, ln1_bias, down_bias, ln2_gain, ln2_bias]))
    half = jnp.asarray(0.5, BF)
    layer_out, gr1, gatt, delta, dwo, dff, sums = feed(
        xt, att, cotangent, out_weight.T, out_weight,
        up_all[:, :, :group], up_all.swapaxes(2, 3), down_all * half, down_all.swapaxes(2, 3) * half, vec,
    )
    everyone = [("dp", dp, 1)] + bits_of("ffn", ffn) + bits_of("dp", dp)[1:]
    parts = 2
    grad_inputs = None
    dws, bsums = [], []
    for index in range(parts):
        grad_inputs, dw, bsum = back(qkv, gatt, xt, gr1, lse, delta, segments, qkv_weight, index, parts, grad_inputs)
        dws.append(dw)
        bsums.append(jnp.sum(bsum, axis=2))
    mine = lax.axis_index("ffn")
    assert ffn == 2
    keep = lax.dynamic_index_in_dim(dff, mine, 0, keepdims=False)
    send = lax.dynamic_index_in_dim(dff, 1 - mine, 0, keepdims=False).astype(BF)
    own = keep + swap(send, "ffn", ffn, 1).astype(F32)
    own = own.reshape(16, -1, part)
    own = sum_over(own, bits_of("dp", dp)).reshape(groups, -1, part)
    dwo = sum_over(dwo.reshape(32, -1, width), everyone).reshape(width, width)
    dqkv = jnp.concatenate(dws, axis=1)
    shape = dqkv.shape
    dqkv = sum_over(dqkv.reshape(32, -1, 384), everyone).reshape(shape)
    small = jnp.concatenate([sums[:6], jnp.concatenate(bsums, axis=1)])
    small = sum_over(small[None], everyone)[0]
    return (
        layer_out,
        grad_inputs,
        dqkv,
        small[6:8],
        dwo,
        small[0],
        small[1],
        small[2],
        own[:, :group],
        own[:, group],
        own[:, group + 16 : 2 * group + 16],
        small[3],
        small[4],
        small[5],
    )


def solution(mesh):
    rows = P(("dp", "ffn"), None)
    shared = P()
    split = P(None, None, "ffn")
    return jax.shard_map(
        partial(per_device, dp=mesh.shape["dp"], ffn=mesh.shape["ffn"]),
        mesh=mesh,
        in_specs=(rows, rows, rows) + (shared,) * 6 + (split, P(None, "ffn"), split) + (shared,) * 3,
        out_specs=(rows, rows) + (shared,) * 6 + (split, P(None, "ffn"), split) + (shared,) * 3,
        check_vma=False,
    )
```

time: 1350 us -> 356 us (0.26); the launches traced: 1330 us -> 356 us
  waiting for transfers between devices: 554 us -> 45.7 us
  matrix products: 440 us -> 0 us
  Pallas kernels: 0 us -> 200 us
  local copies, waits for them, and re-layouts: 162 us -> 25.7 us
  blocking collectives: 73.2 us -> 0 us
  other arithmetic: 87.8 us -> 14.7 us
  starting transfers between devices: 0.25 us -> 55 us
    dot_general x46 -> x0, matrix products: 440 us -> none  [the longest x4 81.5 us: row_backward(): jnp.einsum('hqk,khd->qhd', grad_scores, head_k, preferred_element_type=jn...]
    reduce_scatter x2 -> x0, waiting for transfers between devices: 284 us -> none  [the longest x1 145 us: per_device(): lax.psum_scatter(back_in(row_block, up_full), 'ffn', scatter_dimension=0,...]
    pallas_call x0 -> x4, Pallas kernels: none -> 200 us  [the longest x1 82.3 us: feed(): pl.pallas_call(ffn_kernel, grid=(rows,), in_specs=[per_row, per_row, toke...]
    all_gather x2, waiting for transfers between devices: 163 us -> 0.02 us  [all_parts(): return lax.all_gather(a, 'ffn', axis=0)]
    psum x2 -> x0, waiting for transfers between devices: 107 us -> none  [the longest x1 99.5 us: per_device(): ffn_sums = lax.psum((grad_up_weight, grad_up_bias, grad_down_weight), 'dp')]
    psum x2 -> x0, blocking collectives: 73.2 us -> none  [the longest x1 41.7 us: per_device(): lax.psum((grad_qkv_weight, grad_qv_bias, grad_out_weight, grad_out_bias,...]
    ppermute x0 -> x34, starting transfers between devices: none -> 54.9 us  [swap(): return lax.ppermute(value, axis, [(i, i ^ bit) for i in range(size)])]
    ppermute x0 -> x34, waiting for transfers between devices: none -> 44.9 us  [swap(): return lax.ppermute(value, axis, [(i, i ^ bit) for i in range(size)])]
  transfers between devices with their start and end apart: 6 -> 36, of which waited for: 6 -> 13; matrix products, arithmetic and copies ran while one was open for 5% -> 8% of each run, Pallas kernels for 0% -> 33%
where the time goes in v1:
time: 356 us
  Pallas kernels  200 us (56%)
  starting transfers between devices  55 us (15%)
  waiting for transfers between devices  45.7 us (13%)
  local copies, waits for them, and re-layouts  25.7 us (7%)
  between operations  14.8 us (4%)
  other arithmetic  14.7 us (4%)
    pallas_call x1, Pallas kernels, feed(): pl.pallas_call(ffn_kernel, grid=(rows,), in_specs=[per_row, per_row, toke...  82.3 us
    pallas_call x1, Pallas kernels, attend(): pl.pallas_call(attend_kernel, grid=(rows,), in_specs=[pl.BlockSpec((seq,...  62.8 us
    pallas_call x2, Pallas kernels, back(): pl.pallas_call(partial(back_kernel, head0=index * (chans // HEAD_DIM)), g...  54.9 us
    ppermute x34, starting transfers between devices, swap(): return lax.ppermute(value, axis, [(i, i ^ bit) for i in range(size)])  54.9 us
    ppermute x34, waiting for transfers between devices, swap(): return lax.ppermute(value, axis, [(i, i ^ bit) for i in range(size)])  44.9 us
  transfers between devices with their start and end apart: 36, of which 13 were waited for; matrix products, arithmetic and copies ran while one was open for 8% of the time, Pallas kernels for 33%

profile of v1, /device:TPU:1, one launch (start us, length us, event | category | flops | bytes accessed | tf_op | source)
XLA Modules:
  0.0 355.8 jit_solution(17077506434163345372)
XLA Ops:
  8.8 2.1 maximum_maximum_fusion
  16.3 62.8 %attend.1 = (bf16[4,768,512]{2,1,0:T(8,128)(2,1)}, bf16[4,3,768,512]{3,2,1,0:T(8,128)(2,1)}, bf16[4,768,512]{2,1,0:T(8,128)(2,1)}, f32[4,16,512]{2,1,0:T(8,128)}) custom-call(bf16[2048,768]{1,0:T(8,128)(2,1)} %x_ref.1, s32[4,1,512]{2,1,0:T(1,128)} %reshape.123.seg_ref, bf16[3,4,192,192]{3,2,1,0:T(8,128)(2,1)} %bitcast.44, ...), custom_call_target="tpu_custom_call" | custom-call | tf_op jit(solution)/shard_map/attend/pallas_call | solution.py:93
  85.4 1.8 broadcast_in_dim.22.vec_ref
  87.1 82.3 %feed.1 = (f32[2048,768]{1,0:T(8,128)}, f32[4,768,512]{2,1,0:T(8,128)}, bf16[4,768,512]{2,1,0:T(8,128)(2,1)}, f32[4,16,512]{2,1,0:T(8,128)}, f32[768,768]{1,0:T(...) custom-call(bf16[4,768,512]{2,1,0:T(8,128)(2,1)} %get-tuple-element.31.xt_ref, ...), custom_call_target="tpu_custom_call" | custom-call | tf_op jit(solution)/shard_map/feed/pallas_call | solution.py:289
  170.2 2.2 dynamic-slice_convert_fusion.2
  172.4 27.5 %back.2 = (f32[2048,768]{1,0:T(8,128)}, f32[3,2,192,192]{3,2,1,0:T(8,128)}, f32[2,384,128]{2,1,0:T(8,128)}) custom-call(bf16[4,3,768,512]{3,2,1,0:T(8,128)(2,1)} %get-tuple-element.34.qkv_ref, bf16[4,768,512]{2,1,0:T(8,128)(2,1)} %get-tuple-element.35.gatt_ref, bf16[4,768,512]{2,1,0:T(8,128)(2,1)} %get-tuple-element.31.xt_ref, ...), custom_call_target="tpu_custom_call" | custom-call | tf_op jit(solution)/shard_map/back/pallas_call | solution.py:409
  199.9 27.4 %back.3 = (f32[2048,768]{1,0:T(8,128)}, f32[3,2,192,192]{3,2,1,0:T(8,128)}, f32[2,384,128]{2,1,0:T(8,128)}) custom-call(bf16[4,3,768,512]{3,2,1,0:T(8,128)(2,1)} %get-tuple-element.34.qkv_ref, bf16[4,768,512]{2,1,0:T(8,128)(2,1)} %get-tuple-element.35.gatt_ref, bf16[4,768,512]{2,1,0:T(8,128)(2,1)} %get-tuple-element.31.xt_ref, ...), custom_call_target="tpu_custom_call", output_to_operand_aliasing={{0}: (8, {})} | custom-call | tf_op jit(solution)/shard_map/back/pallas_call | solution.py:409
  229.1 1.9 pad_maximum_fusion
  234.3 2.8 collective-permute-start.11
  237.0 2.0 fusion
  243.5 30.1 %collective-permute-done.1 = bf16[8,36,384]{2,1,0:T(8,128)(2,1)S(1)} collective-permute-done((bf16[8,36,384]{2,1,0:T(8,128)(2,1)S(1)}, bf16[8,36,384]{2,1,0:T(8,128)(2,1)S(1)}, u32[]{:S(2)}, u32[]{:S(2)}) %collective-permute-start.1) | collective-permute-done | bytes 221216 | tf_op jit(solution)/shard_map/ppermute | solution.py:433
  280.6 2.4 collective-permute-start.4
  284.4 2.4 collective-permute-start.5
  288.6 5.8 %collective-permute-start.26 = (bf16[8,104,384]{2,1,0:T(8,128)(2,1)S(1)}, bf16[8,104,384]{2,1,0:T(8,128)(2,1)S(1)}, u32[]{:S(2)}, u32[]{:S(2)}) collective-permute-start(bf16[8,104,384]{2,1,0:T(8,128)(2,1)S(1)} %dynamic-slice_convert_fusion.1), channel_id=1, source_target_pairs={{0,2},{2,0},{4,6},{6,4},{8,10},{10,8},{12,14},{14,12},{16,18},{18,... | collective-permute-start | bytes 1916936 | tf_op jit(solution)/shard_map/ppermute | solution.py:433
  294.5 1.7 collective-permute-start.18
  299.9 1.8 collective-permute-done.19
  302.3 1.8 collective-permute-done.27
  308.8 2.7 collective-permute-start.29
  311.9 1.7 collective-permute-done.29
  313.6 2.9 collective-permute-start.30
  320.1 8.5 %collective-permute-start.9 = (bf16[16,36,384]{2,1,0:T(8,128)(2,1)S(1)}, bf16[16,36,384]{2,1,0:T(8,128)(2,1)S(1)}, u32[]{:S(2)}, u32[]{:S(2)}) collective-permute-start(bf16[16,36,384]{2,1,0:T(8,128)(2,1)S(1)} %maximum_select_fusion.5), channel_id=1, source_target_pairs={{0,2},{2,0},{4,6},{6,4},{8,10},{10,8},{12,14},{14,12},{16,18},{18,... | collective-permute-start | bytes 1327112 | tf_op jit(solution)/shard_map/ppermute | solution.py:433
  330.3 3.5 collective-permute-start.24
  334.7 4.6 %collective-permute-start.33 = (bf16[8,104,384]{2,1,0:T(8,128)(2,1)S(1)}, bf16[8,104,384]{2,1,0:T(8,128)(2,1)}, u32[]{:S(2)}, u32[]{:S(2)}) collective-permute-start(bf16[8,104,384]{2,1,0:T(8,128)(2,1)S(1)} %maximum_select_fusion.3), channel_id=1, source_target_pairs={{0,2},{2,0},{4,6},{6,4},{8,10},{10,8},{12,14},{14,12},{16,18},{18,... | collective-permute-start | bytes 1916936 | tf_op jit(solution)/shard_map/ppermute | solution.py:433
  340.3 1.7 reshape.127
  (176 shorter events, 56.7 us)
Async XLA Ops:
  7.3 71.9 %all-gather.7.cloned.1.call-start = ((), (), s32[]{:S(2)}) async-start(), calls=%async_computation.1 | async-start | bytes 1769472 | tf_op jit(solution)/shard_map/all_gather | solution.py:478
  8.0 74.2 %all-gather.5.cloned.1.call-start = ((), (), s32[]{:S(2)}) async-start(), calls=%async_computation | async-start | bytes 1916928 | tf_op jit(solution)/shard_map/all_gather | solution.py:478
  172.4 102.5 %collective-permute-start.15 = (bf16[16,24,768]{2,1,0:T(8,128)(2,1)}, bf16[16,24,768]{2,1,0:T(8,128)(2,1)}, u32[]{:S(2)}, u32[]{:S(2)}) collective-permute-start(bf16[16,24,768]{2,1,0:T(8,128)(2,1)} %dynamic-slice_convert_fusion.2), channel_id=1, source_target_pairs={{0,2},{2,0},{4,6},{6,4},{8,10},{10,8},{12,14},{14,12},{16,18},{18,... | collective-permute-start | bytes 1769480 | tf_op jit(solution)/shard_map/ppermute | solution.py:433
  228.7 5.5 %collective-permute-start.10 = (bf16[1,8,768]{2,1,0:T(8,128)(2,1)S(1)}, bf16[1,8,768]{2,1,0:T(8,128)(2,1)S(1)}, u32[]{:S(2)}, u32[]{:S(2)}) collective-permute-start(bf16[1,8,768]{2,1,0:T(8,128)(2,1)S(1)} %pad_maximum_fusion.2), channel_id=1, source_target_pairs={{0,2},{2,0},{4,6},{6,4},{8,10},{10,8},{12,14},{14,12},{16,18},{18,... | collective-permute-start | bytes 36872 | tf_op jit(solution)/shard_map/ppermute | solution.py:433
  234.0 6.7 %collective-permute-start = (bf16[16,36,384]{2,1,0:T(8,128)(2,1)S(1)}, bf16[16,36,384]{2,1,0:T(8,128)(2,1)S(1)}, u32[]{:S(2)}, u32[]{:S(2)}) collective-permute-start(bf16[16,36,384]{2,1,0:T(8,128)(2,1)S(1)} %dynamic-slice_convert_fusion.3), channel_id=1, source_target_pairs={{0,2},{2,0},{4,6},{6,4},{8,10},{10,8},{12,14},{14,12},{16,18},{18,... | collective-permute-start | bytes 1327112 | tf_op jit(solution)/shard_map/ppermute | solution.py:433
  239.0 49.1 %collective-permute-start.25 = (bf16[4,416,384]{2,1,0:T(8,128)(2,1)S(1)}, bf16[4,416,384]{2,1,0:T(8,128)(2,1)S(1)}, u32[]{:S(2)}, u32[]{:S(2)}) collective-permute-start(bf16[4,416,384]{2,1,0:T(8,128)(2,1)S(1)} %fusion), channel_id=1, source_target_pairs={{0,1},{1,0},{2,3},{3,2},{4,5},{5,4},{6,7},{7,6},{8,9},{9,8},{10,11... | collective-permute-start | bytes 3833864 | tf_op jit(solution)/shard_map/ppermute | solution.py:433
  240.8 32.7 %collective-permute-start.1 = (bf16[8,36,384]{2,1,0:T(8,128)(2,1)S(1)}, bf16[8,36,384]{2,1,0:T(8,128)(2,1)S(1)}, u32[]{:S(2)}, u32[]{:S(2)}) collective-permute-start(bf16[8,36,384]{2,1,0:T(8,128)(2,1)S(1)} %dynamic-slice_convert_fusion.6), channel_id=1, source_target_pairs={{0,1},{1,0},{2,3},{3,2},{4,5},{5,4},{6,7},{7,6},{8,9},{9,8},{10,11... | collective-permute-start | bytes 663560 | tf_op jit(solution)/shard_map/ppermute | solution.py:433
  242.1 40.9 %collective-permute-start.13 = (bf16[1,8,768]{2,1,0:T(8,128)(2,1)S(1)}, bf16[1,8,768]{2,1,0:T(8,128)(2,1)S(1)}, u32[]{:S(2)}, u32[]{:S(2)}) collective-permute-start(bf16[1,8,768]{2,1,0:T(8,128)(2,1)S(1)} %add_convert_fusion.5), channel_id=1, source_target_pairs={{0,8},{2,10},{4,12},{6,14},{8,0},{10,2},{12,4},{14,6},{16,24},{18,... | collective-permute-start | bytes 36872 | tf_op jit(solution)/shard_map/ppermute | solution.py:433
  278.9 7.9 %collective-permute-start.16 = (bf16[8,24,768]{2,1,0:T(8,128)(2,1)S(1)}, bf16[8,24,768]{2,1,0:T(8,128)(2,1)S(1)}, u32[]{:S(2)}, u32[]{:S(2)}) collective-permute-start(bf16[8,24,768]{2,1,0:T(8,128)(2,1)S(1)} %dynamic-slice_convert_fusion.5), channel_id=1, source_target_pairs={{0,1},{1,0},{2,3},{3,2},{4,5},{5,4},{6,7},{7,6},{8,9},{9,8},{10,11... | collective-permute-start | bytes 884744 | tf_op jit(solution)/shard_map/ppermute | solution.py:433
  283.0 37.0 %collective-permute-start.14 = (bf16[1,8,768]{2,1,0:T(8,128)(2,1)S(1)}, bf16[1,8,768]{2,1,0:T(8,128)(2,1)S(1)}, u32[]{:S(2)}, u32[]{:S(2)}) collective-permute-start(bf16[1,8,768]{2,1,0:T(8,128)(2,1)S(1)} %add_convert_fusion.4), channel_id=1, source_target_pairs={{0,16},{2,18},{4,20},{6,22},{8,24},{10,26},{12,28},{14,30},{16,0},... | collective-permute-start | bytes 36872 | tf_op jit(solution)/shard_map/ppermute | solution.py:433
  284.4 11.8 %collective-permute-start.5 = (bf16[1,36,384]{2,1,0:T(8,128)(2,1)S(1)}, bf16[1,36,384]{2,1,0:T(8,128)(2,1)S(1)}, u32[]{:S(2)}, u32[]{:S(2)}) collective-permute-start(bf16[1,36,384]{2,1,0:T(8,128)(2,1)S(1)} %add_convert_fusion.2), channel_id=1, source_target_pairs={{0,16},{2,18},{4,20},{6,22},{8,24},{10,26},{12,28},{14,30},{16,0},... | collective-permute-start | bytes 82952 | tf_op jit(solution)/shard_map/ppermute | solution.py:433
  286.9 7.5 %collective-permute-start.17 = (bf16[4,24,768]{2,1,0:T(8,128)(2,1)S(1)}, bf16[4,24,768]{2,1,0:T(8,128)(2,1)S(1)}, u32[]{:S(2)}, u32[]{:S(2)}) collective-permute-start(bf16[4,24,768]{2,1,0:T(8,128)(2,1)S(1)} %dynamic-slice_convert_fusion.8), channel_id=1, source_target_pairs={{0,4},{2,6},{4,0},{6,2},{8,12},{10,14},{12,8},{14,10},{16,20},{18,... | collective-permute-start | bytes 442376 | tf_op jit(solution)/shard_map/ppermute | solution.py:433
  288.6 9.4 %collective-permute-start.26 = (bf16[8,104,384]{2,1,0:T(8,128)(2,1)S(1)}, bf16[8,104,384]{2,1,0:T(8,128)(2,1)S(1)}, u32[]{:S(2)}, u32[]{:S(2)}) collective-permute-start(bf16[8,104,384]{2,1,0:T(8,128)(2,1)S(1)} %dynamic-slice_convert_fusion.1), channel_id=1, source_target_pairs={{0,2},{2,0},{4,6},{6,4},{8,10},{10,8},{12,14},{14,12},{16,18},{18,... | collective-permute-start | bytes 1916936 | tf_op jit(solution)/shard_map/ppermute | solution.py:433
  298.2 5.9 %collective-permute-start.27 = (bf16[4,104,384]{2,1,0:T(8,128)(2,1)S(1)}, bf16[4,104,384]{2,1,0:T(8,128)(2,1)S(1)}, u32[]{:S(2)}, u32[]{:S(2)}) collective-permute-start(bf16[4,104,384]{2,1,0:T(8,128)(2,1)S(1)} %dynamic-slice_convert_fusion.4), channel_id=1, source_target_pairs={{0,4},{2,6},{4,0},{6,2},{8,12},{10,14},{12,8},{14,10},{16,20},{18,... | collective-permute-start | bytes 958472 | tf_op jit(solution)/shard_map/ppermute | solution.py:433
  299.4 6.5 %collective-permute-start.7 = (bf16[4,36,384]{2,1,0:T(8,128)(2,1)S(1)}, bf16[4,36,384]{2,1,0:T(8,128)(2,1)S(1)}, u32[]{:S(2)}, u32[]{:S(2)}) collective-permute-start(bf16[4,36,384]{2,1,0:T(8,128)(2,1)S(1)} %maximum_select_fusion.11), channel_id=1, source_target_pairs={{0,4},{2,6},{4,0},{6,2},{8,12},{10,14},{12,8},{14,10},{16,20},{18,... | collective-permute-start | bytes 331784 | tf_op jit(solution)/shard_map/ppermute | solution.py:433
  305.9 14.1 %collective-permute-start.8 = (bf16[8,36,384]{2,1,0:T(8,128)(2,1)S(1)}, bf16[8,36,384]{2,1,0:T(8,128)(2,1)S(1)}, u32[]{:S(2)}, u32[]{:S(2)}) collective-permute-start(bf16[8,36,384]{2,1,0:T(8,128)(2,1)S(1)} %maximum_select_fusion.8), channel_id=1, source_target_pairs={{0,1},{1,0},{2,3},{3,2},{4,5},{5,4},{6,7},{7,6},{8,9},{9,8},{10,11... | collective-permute-start | bytes 663560 | tf_op jit(solution)/shard_map/ppermute | solution.py:433
  306.2 5.3 %collective-permute-start.21 = (bf16[2,24,768]{2,1,0:T(8,128)(2,1)S(1)}, bf16[2,24,768]{2,1,0:T(8,128)(2,1)S(1)}, u32[]{:S(2)}, u32[]{:S(2)}) collective-permute-start(bf16[2,24,768]{2,1,0:T(8,128)(2,1)S(1)} %maximum_select_fusion.12), channel_id=1, source_target_pairs={{0,8},{2,10},{4,12},{6,14},{8,0},{10,2},{12,4},{14,6},{16,24},{18,... | collective-permute-start | bytes 221192 | tf_op jit(solution)/shard_map/ppermute | solution.py:433
  311.5 4.9 %collective-permute-start.22 = (bf16[4,24,768]{2,1,0:T(8,128)(2,1)S(1)}, bf16[4,24,768]{2,1,0:T(8,128)(2,1)S(1)}, u32[]{:S(2)}, u32[]{:S(2)}) collective-permute-start(bf16[4,24,768]{2,1,0:T(8,128)(2,1)S(1)} %maximum_select_fusion.10), channel_id=1, source_target_pairs={{0,4},{2,6},{4,0},{6,2},{8,12},{10,14},{12,8},{14,10},{16,20},{18,... | collective-permute-start | bytes 442376 | tf_op jit(solution)/shard_map/ppermute | solution.py:433
  316.5 13.7 %collective-permute-start.23 = (bf16[8,24,768]{2,1,0:T(8,128)(2,1)S(1)}, bf16[8,24,768]{2,1,0:T(8,128)(2,1)S(1)}, u32[]{:S(2)}, u32[]{:S(2)}) collective-permute-start(bf16[8,24,768]{2,1,0:T(8,128)(2,1)S(1)} %maximum_select_fusion.7), channel_id=1, source_target_pairs={{0,1},{1,0},{2,3},{3,2},{4,5},{5,4},{6,7},{7,6},{8,9},{9,8},{10,11... | collective-permute-start | bytes 884744 | tf_op jit(solution)/shard_map/ppermute | solution.py:433
  318.3 10.3 %collective-permute-start.31 = (bf16[2,104,384]{2,1,0:T(8,128)(2,1)S(1)}, bf16[2,104,384]{2,1,0:T(8,128)(2,1)S(1)}, u32[]{:S(2)}, u32[]{:S(2)}) collective-permute-start(bf16[2,104,384]{2,1,0:T(8,128)(2,1)S(1)} %maximum_select_fusion.9), channel_id=1, source_target_pairs={{0,8},{2,10},{4,12},{6,14},{8,0},{10,2},{12,4},{14,6},{16,24},{18,... | collective-permute-start | bytes 479240 | tf_op jit(solution)/shard_map/ppermute | solution.py:433
  320.1 19.9 %collective-permute-start.9 = (bf16[16,36,384]{2,1,0:T(8,128)(2,1)S(1)}, bf16[16,36,384]{2,1,0:T(8,128)(2,1)S(1)}, u32[]{:S(2)}, u32[]{:S(2)}) collective-permute-start(bf16[16,36,384]{2,1,0:T(8,128)(2,1)S(1)} %maximum_select_fusion.5), channel_id=1, source_target_pairs={{0,2},{2,0},{4,6},{6,4},{8,10},{10,8},{12,14},{14,12},{16,18},{18,... | collective-permute-start | bytes 1327112 | tf_op jit(solution)/shard_map/ppermute | solution.py:433
  328.7 5.9 %collective-permute-start.32 = (bf16[4,104,384]{2,1,0:T(8,128)(2,1)S(1)}, bf16[4,104,384]{2,1,0:T(8,128)(2,1)S(1)}, u32[]{:S(2)}, u32[]{:S(2)}) collective-permute-start(bf16[4,104,384]{2,1,0:T(8,128)(2,1)S(1)} %maximum_select_fusion.6), channel_id=1, source_target_pairs={{0,4},{2,6},{4,0},{6,2},{8,12},{10,14},{12,8},{14,10},{16,20},{18,... | collective-permute-start | bytes 958472 | tf_op jit(solution)/shard_map/ppermute | solution.py:433
  330.3 11.7 %collective-permute-start.24 = (bf16[16,24,768]{2,1,0:T(8,128)(2,1)S(1)}, bf16[16,24,768]{2,1,0:T(8,128)(2,1)}, u32[]{:S(2)}, u32[]{:S(2)}) collective-permute-start(bf16[16,24,768]{2,1,0:T(8,128)(2,1)S(1)} %maximum_select_fusion.4), channel_id=1, source_target_pairs={{0,2},{2,0},{4,6},{6,4},{8,10},{10,8},{12,14},{14,12},{16,18},{18,... | collective-permute-start | bytes 1769480 | tf_op jit(solution)/shard_map/ppermute | solution.py:433
  334.7 10.3 %collective-permute-start.33 = (bf16[8,104,384]{2,1,0:T(8,128)(2,1)S(1)}, bf16[8,104,384]{2,1,0:T(8,128)(2,1)}, u32[]{:S(2)}, u32[]{:S(2)}) collective-permute-start(bf16[8,104,384]{2,1,0:T(8,128)(2,1)S(1)} %maximum_select_fusion.3), channel_id=1, source_target_pairs={{0,2},{2,0},{4,6},{6,4},{8,10},{10,8},{12,14},{14,12},{16,18},{18,... | collective-permute-start | bytes 1916936 | tf_op jit(solution)/shard_map/ppermute | solution.py:433
  (29 other events, 260.3 us)
Sparse Core Ops, SparseCore 0:
  9.6 24.8 all-gather.6
  36.7 24.0 all-gather.4

commit v2 on v1

--- a/solution.py
+++ b/solution.py
@@ -317,17 +317,29 @@
 
 
 def back_kernel(
-    qkv_ref, gatt_ref, xt_ref, gr1_ref, lse_ref, delta_ref, seg_ref, w_ref, *rest, head0
+    core_ref, qkv_ref, gatt_ref, xt_ref, gr1_ref, lse_ref, delta_ref, seg_ref, w_ref, *rest, head0, fresh, final, passed
 ):
-    gin_ref, dw_ref, bsum_ref, qa_ref, ka_ref, va_ref, ga_ref, p_ref, ds_ref, d_ref = rest[-10:]
+    rest = list(rest)
+    if passed:
+        del rest[-12 - passed : -12]
+    if not fresh:
+        dwin_ref, bsin_ref = rest[:2]
+    gin_ref = rest[-12]
+    oa_ref, ob_ref = rest[-11:-9]
+    qa_ref, ka_ref, va_ref, ga_ref, p_ref, ds_ref, d_ref, dw_ref, bsum_ref = rest[-9:]
     chans, seq = xt_ref.shape[1:]
     groups, group = w_ref.shape[1:3]
     first = pl.program_id(0) == 0
+    last = pl.program_id(0) == pl.num_programs(0) - 1
 
     @pl.when(first)
     def _():
-        dw_ref[...] = jnp.zeros_like(dw_ref)
-        bsum_ref[...] = jnp.zeros_like(bsum_ref)
+        if fresh:
+            dw_ref[...] = jnp.zeros_like(dw_ref)
+            bsum_ref[...] = jnp.zeros_like(bsum_ref)
+        else:
+            dw_ref[...] = dwin_ref[...]
+            bsum_ref[...] = bsin_ref[...]
 
     seg = seg_ref[0]
     rank = lax.broadcasted_iota(jnp.int32, (16, seq), 0)
@@ -383,87 +395,148 @@
         parts.append(total)
     gin_ref[...] = jnp.concatenate(parts, axis=0).T
 
-
-def back(qkv, gatt, xt, gr1, lse, delta, seg, w, index, parts, into):
+    if not final:
+        @pl.when(last)
+        def _():
+            oa_ref[...] = dw_ref[...]
+            ob_ref[...] = bsum_ref[...]
+
+    else:
+        @pl.when(last)
+        def _():
+            half = PACK // 2
+            core = core_ref[0]
+
+            def put(row, value):
+                rows = value.shape[0]
+                where = row // half
+                at = slice(row % half, row % half + rows)
+
+                @pl.when(core == where)
+                def _():
+                    oa_ref[at, :] = value
+
+                @pl.when(core != where)
+                def _():
+                    ob_ref[at, :] = value.astype(BF)
+
+            tiles = chans // 128
+            bias = jnp.concatenate([jnp.sum(bsum_ref[n].T, axis=0, keepdims=True) for n in range(2)], axis=0)
+            bias = jnp.concatenate([bias, jnp.zeros((6, chans), F32)], axis=0)
+            for j in range(3):
+                both = jnp.concatenate([dw_ref[j, g] for g in range(groups)], axis=1)
+                for c in range(tiles):
+                    for a in range(0, group, 64):
+                        put(c * 3 * group + j * group + a, both[a : a + 64, c * 128 : c * 128 + 128])
+            for c in range(tiles):
+                put(tiles * 3 * group + 8 * c, bias[:, c * 128 : c * 128 + 128])
+            for row in range(tiles * 3 * group + 8 * tiles, PACK, 8):
+                put(row, jnp.zeros((8, 128), F32))
+
+
+PACK = 1792
+
+
+def back(core, qkv, gatt, xt, gr1, lse, delta, seg, w, index, parts, row0, count, carried, into, final, sends, keeps):
     rows, _, width, seq = qkv.shape
     chans = width // parts
     groups, group = w.shape[1] // parts, w.shape[2]
-    per_row = pl.BlockSpec((1, chans, seq), lambda r: (r, index, 0))
-    full = pl.BlockSpec((1, 16, seq), lambda r: (r, 0, 0))
+    per_row = pl.BlockSpec((1, chans, seq), lambda r: (r + row0, index, 0))
+    full = pl.BlockSpec((1, 16, seq), lambda r: (r + row0, 0, 0))
     in_specs = [
-        pl.BlockSpec((1, 3, chans, seq), lambda r: (r, 0, index, 0)),
+        pl.BlockSpec(memory_space=pltpu.SMEM),
+        pl.BlockSpec((1, 3, chans, seq), lambda r: (r + row0, 0, index, 0)),
         per_row,
         per_row,
         per_row,
         full,
         full,
-        pl.BlockSpec((1, 1, seq), lambda r: (r, 0, 0)),
+        pl.BlockSpec((1, 1, seq), lambda r: (r + row0, 0, 0)),
         pl.BlockSpec((3, groups, group, group), lambda r: (0, index, 0, 0)),
     ]
-    args = [qkv, gatt, xt, gr1, lse, delta, seg.reshape(rows, 1, seq), w]
+    args = [core, qkv, gatt, xt, gr1, lse, delta, seg.reshape(rows, 1, seq), w]
+    sums = [jax.ShapeDtypeStruct((3, groups, group, group), F32), jax.ShapeDtypeStruct((2, chans, 128), F32)]
+    if carried is not None:
+        in_specs += [pl.BlockSpec((3, groups, group, group), lambda r: (0, 0, 0, 0)), pl.BlockSpec((2, chans, 128), lambda r: (0, 0, 0))]
+        args += list(carried)
     alias = {}
     if into is not None:
         in_specs.append(pl.BlockSpec(memory_space=pl.ANY))
         args.append(into)
-        alias = {len(args) - 1: 0}
+        alias = {len(args) - 1: len(keeps)}
+    for n, value in enumerate(keeps):
+        alias[len(args)] = n
+        in_specs.append(pl.BlockSpec(memory_space=pl.ANY))
+        args.append(value)
+    for value in sends:
+        in_specs.append(pl.BlockSpec(memory_space=pl.ANY))
+        args.append(value)
+    if final:
+        outs = [jax.ShapeDtypeStruct((PACK // 2, 128), F32), jax.ShapeDtypeStruct((PACK // 2, 128), BF)]
+    else:
+        outs = sums
     return pl.pallas_call(
-        partial(back_kernel, head0=index * (chans // HEAD_DIM)),
-        grid=(rows,),
+        partial(back_kernel, head0=index * (chans // HEAD_DIM), fresh=carried is None, final=final, passed=len(keeps)),
+        grid=(count,),
         in_specs=in_specs,
-        out_specs=[
-            pl.BlockSpec((seq, chans), lambda r: (r, index)),
-            pl.BlockSpec((3, groups, group, group), lambda r: (0, 0, 0, 0)),
-            pl.BlockSpec((2, chans, 128), lambda r: (0, 0, 0)),
-        ],
-        out_shape=[
-            jax.ShapeDtypeStruct((rows * seq, width), F32),
-            jax.ShapeDtypeStruct((3, groups, group, group), F32),
-            jax.ShapeDtypeStruct((2, chans, 128), F32),
-        ],
+        out_specs=[pl.BlockSpec(memory_space=pl.ANY) for _ in keeps]
+        + [pl.BlockSpec((seq, chans), lambda r: (r + row0, index))]
+        + [pl.BlockSpec(o.shape, lambda r, n=len(o.shape): (0,) * n) for o in outs],
+        out_shape=[jax.ShapeDtypeStruct(value.shape, value.dtype) for value in keeps]
+        + [jax.ShapeDtypeStruct((rows * seq, width), F32)]
+        + outs,
         scratch_shapes=[pltpu.VMEM((80, seq), BF) for _ in range(4)]
         + [pltpu.VMEM((seq // 256, seq, 256), BF) for _ in range(2)]
-        + [pltpu.VMEM((3, chans, seq), BF)],
+        + [pltpu.VMEM((3, chans, seq), BF)]
+        + [pltpu.VMEM(o.shape, F32) for o in sums],
         input_output_aliases=alias,
         compiler_params=params("arbitrary"),
+        cost_estimate=pl.CostEstimate(flops=int(7e9 * count / 2), transcendentals=0, bytes_accessed=20 * 2**20),
         name="back",
     )(*args)
 
 
-def swap(value, axis, size, bit):
-    return lax.ppermute(value, axis, [(i, i ^ bit) for i in range(size)])
-
-
-def scatter(value, axis, size, bit):
-    half = value.shape[0] // 2
-    mine = (lax.axis_index(axis) // bit) % 2
-    keep = lax.dynamic_slice_in_dim(value, mine * half, half, 0)
-    send = lax.dynamic_slice_in_dim(value, (1 - mine) * half, half, 0).astype(BF)
-    return keep + swap(send, axis, size, bit).astype(F32)
-
-
-def gather(value, axis, size, bit):
-    mine = (lax.axis_index(axis) // bit) % 2
-    other = swap(value, axis, size, bit)
-    return jnp.where(mine == 0, jnp.concatenate([value, other]), jnp.concatenate([other, value]))
-
-
-def sum_over(value, steps):
-    done = []
-    for axis, size, bit in steps:
-        if value.shape[0] % 2 == 0:
-            value = scatter(value, axis, size, bit)
-            done.append((axis, size, bit))
-        else:
-            low = value.astype(BF)
-            value = low.astype(F32) + swap(low, axis, size, bit).astype(F32)
+class Axis:
+    def __init__(self, name, size, bit):
+        self.name, self.pairs = name, [(i, i ^ bit) for i in range(size)]
+        self.side = (lax.axis_index(name) // bit) % 2
+
+    def swap(self, value):
+        return lax.ppermute(value, self.name, self.pairs)
+
+    def split(self, value):
+        half = value.shape[0] // 2
+        keep = lax.dynamic_slice_in_dim(value, self.side * half, half, 0)
+        send = lax.dynamic_slice_in_dim(value, (1 - self.side) * half, half, 0)
+        return keep, send.astype(BF)
+
+    def join(self, value):
+        other = self.swap(value)
+        return jnp.where(self.side == 0, jnp.concatenate([value, other]), jnp.concatenate([other, value]))
+
+
+def add(keep, got):
+    return keep + got.astype(F32)
+
+
+def sum_down(value, axes):
+    for axis in axes:
+        keep, send = axis.split(value)
+        value = add(keep, axis.swap(send))
+    return value
+
+
+def sum_across(value, axes):
     low = value.astype(BF)
-    for step in reversed(done):
-        low = gather(low, *step)
-    return low.astype(F32)
-
-
-def bits_of(axis, size):
-    return [(axis, size, 1 << k) for k in range(size.bit_length() - 1)]
+    for axis in axes:
+        low = (low.astype(F32) + axis.swap(low).astype(F32)).astype(BF)
+    return low
+
+
+def gather_up(low, axes):
+    for axis in reversed(axes):
+        low = axis.join(low)
+    return low
 
 
 def per_device(
@@ -473,15 +546,16 @@
     width = inputs.shape[1]
     groups, group = qkv_weight.shape[1:3]
     part = up_weight.shape[2]
-
-    def all_parts(a):
-        return lax.all_gather(a, "ffn", axis=0)
+    assert ffn == 2
+    bits = [Axis("dp", dp, 1 << k) for k in range(dp.bit_length() - 1)]
+    core, ax, rest = bits[0], bits[1], bits[2:]
+    ay = Axis("ffn", ffn, 1)
 
     up_aug = jnp.concatenate(
         [up_weight, up_bias[:, None, :], jnp.zeros((groups, 15, part), BF)], axis=1
     )
-    up_all = all_parts(up_aug)
-    down_all = all_parts(down_weight)
+    up_all = lax.all_gather(up_aug, "ffn", axis=0)
+    down_all = lax.all_gather(down_weight, "ffn", axis=0)
 
     def lanes(v):
         return jnp.broadcast_to(v[..., None], v.shape + (128,))
@@ -494,32 +568,66 @@
         xt, att, cotangent, out_weight.T, out_weight,
         up_all[:, :, :group], up_all.swapaxes(2, 3), down_all * half, down_all.swapaxes(2, 3) * half, vec,
     )
-    everyone = [("dp", dp, 1)] + bits_of("ffn", ffn) + bits_of("dp", dp)[1:]
+    dff = lax.dynamic_update_slice(
+        dff, jnp.broadcast_to(sums[:6].reshape(1, 1, 12, part), (2, 1, 12, part)), (0, 0, 2 * group + 16, 0)
+    )
+
+    core_id = core.side.astype(jnp.int32).reshape(1)
+    rows = segments.shape[0]
+    step = max(rows // 2, 1)
     parts = 2
-    grad_inputs = None
-    dws, bsums = [], []
-    for index in range(parts):
-        grad_inputs, dw, bsum = back(qkv, gatt, xt, gr1, lse, delta, segments, qkv_weight, index, parts, grad_inputs)
-        dws.append(dw)
-        bsums.append(jnp.sum(bsum, axis=2))
-    mine = lax.axis_index("ffn")
-    assert ffn == 2
-    keep = lax.dynamic_index_in_dim(dff, mine, 0, keepdims=False)
-    send = lax.dynamic_index_in_dim(dff, 1 - mine, 0, keepdims=False).astype(BF)
-    own = keep + swap(send, "ffn", ffn, 1).astype(F32)
-    own = own.reshape(16, -1, part)
-    own = sum_over(own, bits_of("dp", dp)).reshape(groups, -1, part)
-    dwo = sum_over(dwo.reshape(32, -1, width), everyone).reshape(width, width)
-    dqkv = jnp.concatenate(dws, axis=1)
-    shape = dqkv.shape
-    dqkv = sum_over(dqkv.reshape(32, -1, 384), everyone).reshape(shape)
-    small = jnp.concatenate([sums[:6], jnp.concatenate(bsums, axis=1)])
-    small = sum_over(small[None], everyone)[0]
+    state = {"grad_inputs": None, "carried": None}
+    packs = []
+
+    def under(call, *stages):
+        keeps, sends = [keep for _, keep, _ in stages], [send for _, _, send in stages]
+        got = [axis.swap(send) for axis, _, send in stages]
+        if call is not None:
+            index, row0 = call
+            final = row0 + step >= rows
+            outs = back(
+                core_id, qkv, gatt, xt, gr1, lse, delta, segments, qkv_weight, index, parts, row0, step,
+                state["carried"], state["grad_inputs"], final, sends, keeps,
+            )
+            keeps, (state["grad_inputs"], *carried) = outs[: len(keeps)], outs[len(keeps) :]
+            state["carried"] = None if final else carried
+            if final:
+                packs.append(carried)
+        return [add(keep, arrived) for keep, arrived in zip(keeps, got)]
+
+    calls = [(index, row0) for index in range(parts) for row0 in range(0, rows, step)]
+    calls += [None] * (4 - len(calls))
+    ffn1, out1 = under(calls[0], (core, *core.split(dff.swapaxes(0, 1))), (core, *core.split(dwo)))
+    ffn2, out2 = under(calls[1], (ay, *ay.split(ffn1.swapaxes(0, 1))), (ax, *ax.split(out1)))
+    ffn3, out3, sum0 = under(calls[2], (ax, *ax.split(ffn2[0])), (ay, *ay.split(out2)), (core, *packs[0]))
+    low, olow = ffn3.astype(BF), out3.astype(BF)
+    ffn4, out4, sum0 = under(
+        calls[3], (rest[0], low.astype(F32), low), (rest[0], olow.astype(F32), olow), (ay, *ay.split(sum0))
+    )
+    own = gather_up(sum_across(ffn4, rest[1:]), [core, ax]).astype(F32)
+    dwo = gather_up(sum_across(out4, rest[1:]), [core, ax, ay]).astype(F32)
+    grad_inputs = state["grad_inputs"]
+    totals = [gather_up(sum_across(sum_down(sum0, [ax]), rest), [core, ay, ax])]
+    pkeep, psend = packs[1]
+    first = add(pkeep, core.swap(psend))
+    totals.append(gather_up(sum_across(sum_down(first, [ay, ax]), rest), [core, ay, ax]))
+    grads, biases = [], []
+    for total in totals:
+        total = total.astype(F32)
+        tiles = width // parts // 128
+        body = total[: tiles * 3 * group].reshape(tiles, 3, group, 128).transpose(1, 2, 0, 3)
+        body = body.reshape(3, group, groups // parts, group).swapaxes(1, 2)
+        grads.append(body)
+        tail = total[tiles * 3 * group : tiles * 3 * group + 8 * tiles].reshape(tiles, 8, 128)[:, :2]
+        biases.append(tail.transpose(1, 0, 2).reshape(2, -1))
+    dqkv = jnp.concatenate(grads, axis=1)
+    qvb = jnp.concatenate(biases, axis=1)
+    small = own[0, 2 * group + 16 : 2 * group + 28].reshape(6, width)
     return (
         layer_out,
         grad_inputs,
         dqkv,
-        small[6:8],
+        qvb,
         dwo,
         small[0],
         small[1],
@@ -544,3 +652,15 @@
         out_specs=(rows, rows) + (shared,) * 6 + (split, P(None, "ffn"), split) + (shared,) * 3,
         check_vma=False,
     )
+
+
+def specs(which):
+    bf, f, i = jnp.bfloat16, jnp.float32, jnp.int32
+    if which == "attend":
+        return attend, [((2048, 768), bf), ((4, 512), i), ((3, 4, 192, 192), bf), ((3, 768, 128), f)]
+    if which == "feed":
+        return feed, [((4, 768, 512), bf), ((4, 768, 512), bf), ((2048, 768), bf), ((768, 768), bf), ((768, 768), bf), ((2, 4, 192, 384), bf),
+                      ((2, 4, 384, 208), bf), ((2, 4, 192, 384), bf), ((2, 4, 384, 192), bf), ((6, 768, 128), f)]
+    if which == "back":
+        return (lambda *a: back(*a, 0, 2, None)), [((4, 3, 768, 512), bf), ((4, 768, 512), bf), ((4, 768, 512), bf), ((4, 768, 512), f),
+                                                   ((4, 16, 512), f), ((4, 16, 512), f), ((4, 512), i), ((3, 4, 192, 192), bf)]

time: 356 us -> 353 us (level)
  waiting for transfers between devices: 45.7 us -> 22 us
  local copies, waits for them, and re-layouts: 25.7 us -> 38.5 us
  Pallas kernels: 200 us -> 209 us
  starting transfers between devices: 55 us -> 46.6 us
  other arithmetic: 14.7 us -> 21.4 us
    ppermute x34 -> x31, waiting for transfers between devices: 44.9 us -> 21.2 us  [swap(): return lax.ppermute(value, self.name, self.pairs)]
    pallas_call x2 -> x4, Pallas kernels: 54.9 us -> 63.8 us  [back(): pl.pallas_call(partial(back_kernel, head0=index * (chans // HEAD_DIM), fr...]
    ppermute x34 -> x31, starting transfers between devices: 54.9 us -> 46.6 us  [swap(): return lax.ppermute(value, self.name, self.pairs)]
    dynamic_slice x0 -> x8, local copies, waits for them, and re-layouts: none -> 7.29 us  [split(): keep = lax.dynamic_slice_in_dim(value, self.side * half, half, 0)]
    convert_element_type x11 -> x16, other arithmetic: 2.14 us -> 7.61 us  [the longest x1 3.35 us: per_device(): dwo = gather_up(sum_across(out4, rest[1:]), [core, ax, ay]).astype(F32)]
    unnamed x37 -> x66, local copies, waits for them, and re-layouts: 3.6 us -> 8.3 us
    convert_element_type x16 -> x11, local copies, waits for them, and re-layouts: 7.47 us -> 3.5 us  [split(): return (keep, send.astype(BF))]
    squeeze x0 -> x6, local copies, waits for them, and re-layouts: none -> 3.6 us  [the longest x1 0.6 us: per_device(): small[3]]
  transfers between devices with their start and end apart: 36 -> 33, of which waited for: 13 -> 9; matrix products, arithmetic and copies ran while one was open for 8% -> 11% of each run, Pallas kernels for 33% -> 36%
where the time goes in v2:
time: 353 us; the launch traced here: 352 us
  Pallas kernels  209 us (59%)
  starting transfers between devices  46.6 us (13%)
  local copies, waits for them, and re-layouts  38.5 us (11%)
  waiting for transfers between devices  22 us (6%)
  other arithmetic  21.4 us (6%)
  between operations  14.9 us (4%)
    pallas_call x1, Pallas kernels, feed(): pl.pallas_call(ffn_kernel, grid=(rows,), in_specs=[per_row, per_row, toke...  82.3 us
    pallas_call x4, Pallas kernels, back(): pl.pallas_call(partial(back_kernel, head0=index * (chans // HEAD_DIM), fr...  63.8 us
    pallas_call x1, Pallas kernels, attend(): pl.pallas_call(attend_kernel, grid=(rows,), in_specs=[pl.BlockSpec((seq,...  63 us
    ppermute x31, starting transfers between devices, swap(): return lax.ppermute(value, self.name, self.pairs)  46.6 us
    ppermute x31, waiting for transfers between devices, swap(): return lax.ppermute(value, self.name, self.pairs)  21.2 us
    unnamed x66, local copies, waits for them, and re-layouts  8.3 us
    dynamic_slice x8, local copies, waits for them, and re-layouts, split(): keep = lax.dynamic_slice_in_dim(value, self.side * half, half, 0)  7.29 us
  transfers between devices with their start and end apart: 33, of which 9 were waited for; matrix products, arithmetic and copies ran while one was open for 11% of the time, Pallas kernels for 36%

profile of v2, /device:TPU:1, one launch (start us, length us, event | category | flops | bytes accessed | tf_op | source)
XLA Modules:
  0.0 352.5 jit_solution(14195568711005188362)
XLA Ops:
  8.8 2.1 maximum_maximum_fusion
  16.3 63.0 %attend.1 = (bf16[4,768,512]{2,1,0:T(8,128)(2,1)}, bf16[4,3,768,512]{3,2,1,0:T(8,128)(2,1)}, bf16[4,768,512]{2,1,0:T(8,128)(2,1)}, f32[4,16,512]{2,1,0:T(8,128)}) custom-call(bf16[2048,768]{1,0:T(8,128)(2,1)} %x_ref.1, s32[4,1,512]{2,1,0:T(1,128)} %reshape.107.seg_ref, bf16[3,4,192,192]{3,2,1,0:T(8,128)(2,1)} %bitcast.62, ...), custom_call_target="tpu_custom_call" | custom-call | tf_op jit(solution)/shard_map/attend/pallas_call | solution.py:93
  85.6 1.8 broadcast_in_dim.28.vec_ref
  87.3 82.3 %feed.1 = (f32[2048,768]{1,0:T(8,128)}, f32[4,768,512]{2,1,0:T(8,128)}, bf16[4,768,512]{2,1,0:T(8,128)(2,1)}, f32[4,16,512]{2,1,0:T(8,128)}, f32[768,768]{1,0:T(...) custom-call(bf16[4,768,512]{2,1,0:T(8,128)(2,1)} %get-tuple-element.47.xt_ref, ...), custom_call_target="tpu_custom_call" | custom-call | tf_op jit(solution)/shard_map/feed/pallas_call | solution.py:289
  171.9 2.0 fusion
  175.6 1.7 copy.90.rest_0_
  179.6 15.6 %back.4 = (f32[2,2,416,384]{3,2,1,0:T(8,128)}, f32[384,768]{1,0:T(8,128)}, f32[2048,768]{1,0:T(8,128)}, f32[3,2,192,192]{3,2,1,0:T(8,128)}, f32[2,384,128]{2,1,0:T(8,128)}) custom-call(s32[1]{0:T(128)} %bitcast.8.core_ref, bf16[4,3,768,512]{3,2,1,0:T(8,128)(2,1)} %get-tuple-element.50.qkv_ref, ...), custom_call_target="tpu_custom_call", output_to_operand_aliasing={{0}: (9, {}), {1}: (10, {})} | custom-call | flops 7000000000 | bytes 20971520 | tf_op jit(solution)/shard_map/back/pallas_call | solution.py:478
  196.8 2.8 collective-permute-start.3
  203.3 16.3 %back.5 = (f32[1,2,416,384]{3,2,1,0:T(8,128)}, f32[192,768]{1,0:T(8,128)}, f32[2048,768]{1,0:T(8,128)}, f32[896,128]{1,0:T(8,128)}, bf16[896,128]{1,0:T(8,128)(2,1)}) custom-call(s32[1]{0:T(128)} %bitcast.8.core_ref, bf16[4,3,768,512]{3,2,1,0:T(8,128)(2,1)} %get-tuple-element.50.qkv_ref, ...), custom_call_target="tpu_custom_call", output_to_operand_aliasing={{2}: (11, {}), {0}: (12, {}), {1}: (13, {})} | custom-call | flops 7000000000 | bytes 20971520 | tf_op jit(solution)/shard_map/back/pallas_call | solution.py:478
  225.0 15.5 %back.6 = (f32[1,416,384]{2,1,0:T(8,128)}, f32[96,768]{1,0:T(8,128)}, f32[896,128]{1,0:T(8,128)}, f32[2048,768]{1,0:T(8,128)}, f32[3,2,192,192]{3,2,1,0:T(8,128)}, /*index=5*/f32[2,384,128]{2,1,0:T(8,128)}) custom-call(s32[1]{0:T(128)} %bitcast.8.core_ref, ...), custom_call_target="tpu_custom_call", output_to_operand_aliasing={{3}: (9, {}), {0}: (10, {}), {1}: (11, {}), {2}: (12, {})} | custom-call | flops 7000000000 | bytes 20971520 | tf_op jit(solution)/shard_map/back/pallas_call | solution.py:478
  245.4 16.4 %back.7 = (f32[1,416,384]{2,1,0:T(8,128)}, f32[96,768]{1,0:T(8,128)}, f32[448,128]{1,0:T(8,128)}, f32[2048,768]{1,0:T(8,128)}, f32[896,128]{1,0:T(8,128)}, /*index=5*/bf16[896,128]{1,0:T(8,128)(2,1)}) custom-call(s32[1]{0:T(128)} %bitcast.8.core_ref, ...), custom_call_target="tpu_custom_call", output_to_operand_aliasing={{3}: (11, {}), {0}: (12, {}), {1}: (13, {}), {2}: (14, {})} | custom-call | flops 7000000000 | bytes 20971520 | tf_op jit(solution)/shard_map/back/pallas_call | solution.py:478
  269.3 2.4 collective-permute-start.23
  271.7 7.8 %collective-permute-done.9 = bf16[224,128]{1,0:T(8,128)(2,1)S(1)} collective-permute-done((bf16[224,128]{1,0:T(8,128)(2,1)S(1)}, bf16[224,128]{1,0:T(8,128)(2,1)S(1)}, u32[]{:S(2)}, u32[]{:S(2)}) %collective-permute-start.9) | collective-permute-done | bytes 57376 | tf_op jit(solution)/shard_map/ppermute | solution.py:505
  281.0 2.6 collective-permute-done.10
  285.2 1.8 collective-permute-done.11
  290.3 1.7 collective-permute-done.16
  292.0 2.2 collective-permute-start.17
  294.3 4.8 %collective-permute-start.13 = (bf16[896,128]{1,0:T(8,128)(2,1)S(1)}, bf16[896,128]{1,0:T(8,128)(2,1)S(1)}, u32[]{:S(2)}, u32[]{:S(2)}) collective-permute-start(bf16[896,128]{1,0:T(8,128)(2,1)S(1)} %maximum_select_fusion.7), channel_id=1, source_target_pairs={{0,2},{2,0},{4,6},{6,4},{8,10},{10,8},{12,14},{14,12},{16,18},{18,... | collective-permute-start | bytes 688136 | tf_op jit(solution)/shard_map/ppermute | solution.py:505
  304.8 1.9 collective-permute-done.19
  308.8 10.9 %collective-permute-start.26 = (bf16[384,768]{1,0:T(8,128)(2,1)}, bf16[384,768]{1,0:T(8,128)(2,1)}, u32[]{:S(2)}, u32[]{:S(2)}) collective-permute-start(bf16[384,768]{1,0:T(8,128)(2,1)} %maximum_select_fusion.3), channel_id=1, source_target_pairs={{0,2},{2,0},{4,6},{6,4},{8,10},{10,8},{12,14},{14,12},{16,18},{18,... | collective-permute-start | bytes 1769480 | tf_op jit(solution)/shard_map/ppermute | solution.py:505
  319.8 2.7 collective-permute-start.21
  328.1 2.1 copy.97
  330.2 2.5 collective-permute-done.29
  336.3 3.3 fusion.2
  (210 shorter events, 71.2 us)
Async XLA Ops:
  7.2 72.1 %all-gather.7.cloned.1.call-start = ((), (), s32[]{:S(2)}) async-start(), calls=%async_computation.1 | async-start | bytes 1769472 | tf_op jit(solution)/shard_map/all_gather | solution.py:558
  7.9 74.4 %all-gather.5.cloned.1.call-start = ((), (), s32[]{:S(2)}) async-start(), calls=%async_computation | async-start | bytes 1916928 | tf_op jit(solution)/shard_map/all_gather | solution.py:557
  175.1 25.3 %collective-permute-start = (bf16[2,2,416,384]{3,2,0,1:T(8,128)(2,1)S(1)}, bf16[2,2,416,384]{3,2,0,1:T(8,128)(2,1)S(1)}, u32[]{:S(2)}, u32[]{:S(2)}) collective-permute-start(bf16[2,2,416,384]{3,2,0,1:T(8,128)(2,1)S(1)} %fusion), channel_id=1, source_target_pairs={{0,2},{2,0},{4,6},{6,4},{8,10},{10,8},{12,14},{14,12},{16,18},{18,... | collective-permute-start | bytes 3833864 | tf_op jit(solution)/shard_map/ppermute | solution.py:505
  178.3 16.9 %collective-permute-start.1 = (bf16[384,768]{1,0:T(8,128)(2,1)S(1)}, bf16[384,768]{1,0:T(8,128)(2,1)S(1)}, u32[]{:S(2)}, u32[]{:S(2)}) collective-permute-start(bf16[384,768]{1,0:T(8,128)(2,1)S(1)} %dynamic-slice_convert_fusion.2.rest_3_), channel_id=1, source_target_pairs={{0,2},{2,0},{4,6},{6,4},{8,10},{10,8},{12,14},{14,12},{16,18},{18,... | collective-permute-start | bytes 1769480 | tf_op jit(solution)/shard_map/ppermute | solution.py:505
  196.8 22.9 %collective-permute-start.3 = (bf16[192,768]{1,0:T(8,128)(2,1)S(1)}, bf16[192,768]{1,0:T(8,128)(2,1)S(1)}, u32[]{:S(2)}, u32[]{:S(2)}) collective-permute-start(bf16[192,768]{1,0:T(8,128)(2,1)S(1)} %dynamic-slice_convert_fusion.4.rest_6_), channel_id=1, source_target_pairs={{0,4},{2,6},{4,0},{6,2},{8,12},{10,14},{12,8},{14,10},{16,20},{18,... | collective-permute-start | bytes 884744 | tf_op jit(solution)/shard_map/ppermute | solution.py:505
  202.0 21.2 %collective-permute-start.2 = (bf16[1,2,416,384]{3,2,1,0:T(8,128)(2,1)S(1)}, bf16[1,2,416,384]{3,2,1,0:T(8,128)(2,1)S(1)}, u32[]{:S(2)}, u32[]{:S(2)}) collective-permute-start(bf16[1,2,416,384]{3,2,1,0:T(8,128)(2,1)S(1)} %fusion.3.rest_5_), channel_id=1, source_target_pairs={{0,1},{1,0},{2,3},{3,2},{4,5},{5,4},{6,7},{7,6},{8,9},{9,8},{10,11... | collective-permute-start | bytes 1916936 | tf_op jit(solution)/shard_map/ppermute | solution.py:505
  220.9 22.6 %collective-permute-start.5 = (bf16[96,768]{1,0:T(8,128)(2,1)S(1)}, bf16[96,768]{1,0:T(8,128)(2,1)S(1)}, u32[]{:S(2)}, u32[]{:S(2)}) collective-permute-start(bf16[96,768]{1,0:T(8,128)(2,1)S(1)} %dynamic-slice_convert_fusion.5.rest_5_), channel_id=1, source_target_pairs={{0,1},{1,0},{2,3},{3,2},{4,5},{5,4},{6,7},{7,6},{8,9},{9,8},{10,11... | collective-permute-start | bytes 442376 | tf_op jit(solution)/shard_map/ppermute | solution.py:505
  221.7 18.8 %collective-permute-start.6 = (bf16[896,128]{1,0:T(8,128)(2,1)S(1)}, bf16[896,128]{1,0:T(8,128)(2,1)S(1)}, u32[]{:S(2)}, u32[]{:S(2)}) collective-permute-start(bf16[896,128]{1,0:T(8,128)(2,1)S(1)} %copy-done.21), channel_id=1, source_target_pairs={{0,2},{2,0},{4,6},{6,4},{8,10},{10,8},{12,14},{14,12},{16,18},{18,... | collective-permute-start | bytes 688136 | tf_op jit(solution)/shard_map/ppermute | solution.py:505
  224.3 20.0 %collective-permute-start.4 = (bf16[1,416,384]{2,1,0:T(8,128)(2,1)S(1)}, bf16[1,416,384]{2,1,0:T(8,128)(2,1)S(1)}, u32[]{:S(2)}, u32[]{:S(2)}) collective-permute-start(bf16[1,416,384]{2,1,0:T(8,128)(2,1)S(1)} %fusion.6.rest_4_), channel_id=1, source_target_pairs={{0,4},{2,6},{4,0},{6,2},{8,12},{10,14},{12,8},{14,10},{16,20},{18,... | collective-permute-start | bytes 958472 | tf_op jit(solution)/shard_map/ppermute | solution.py:505
  241.8 20.1 %collective-permute-start.7 = (bf16[448,128]{1,0:T(8,128)(2,1)S(1)}, bf16[448,128]{1,0:T(8,128)(2,1)S(1)}, u32[]{:S(2)}, u32[]{:S(2)}) collective-permute-start(bf16[448,128]{1,0:T(8,128)(2,1)S(1)} %dynamic-slice_convert_fusion.7.rest_8_), channel_id=1, source_target_pairs={{0,1},{1,0},{2,3},{3,2},{4,5},{5,4},{6,7},{7,6},{8,9},{9,8},{10,11... | collective-permute-start | bytes 344072 | tf_op jit(solution)/shard_map/ppermute | solution.py:505
  265.1 35.6 %collective-permute-start.27 = (bf16[1,416,384]{2,1,0:T(8,128)(2,1)S(1)}, bf16[1,416,384]{2,1,0:T(8,128)(2,1)S(1)}, u32[]{:S(2)}, u32[]{:S(2)}) collective-permute-start(bf16[1,416,384]{2,1,0:T(8,128)(2,1)S(1)} %copy-done.14), channel_id=1, source_target_pairs={{0,8},{2,10},{4,12},{6,14},{8,0},{10,2},{12,4},{14,6},{16,24},{18,... | collective-permute-start | bytes 958472 | tf_op jit(solution)/shard_map/ppermute | solution.py:505
  265.3 19.3 %collective-permute-start.14 = (bf16[896,128]{1,0:T(8,128)(2,1)}, bf16[896,128]{1,0:T(8,128)(2,1)S(1)}, u32[]{:S(2)}, u32[]{:S(2)}) collective-permute-start(bf16[896,128]{1,0:T(8,128)(2,1)} %get-tuple-element.77), channel_id=1, source_target_pairs={{0,2},{2,0},{4,6},{6,4},{8,10},{10,8},{12,14},{14,12},{16,18},{18,... | collective-permute-start | bytes 688136 | tf_op jit(solution)/shard_map/ppermute | solution.py:505
  266.7 12.9 %collective-permute-start.9 = (bf16[224,128]{1,0:T(8,128)(2,1)S(1)}, bf16[224,128]{1,0:T(8,128)(2,1)S(1)}, u32[]{:S(2)}, u32[]{:S(2)}) collective-permute-start(bf16[224,128]{1,0:T(8,128)(2,1)S(1)} %add_convert_fusion.11), channel_id=1, source_target_pairs={{0,8},{2,10},{4,12},{6,14},{8,0},{10,2},{12,4},{14,6},{16,24},{18,... | collective-permute-start | bytes 172040 | tf_op jit(solution)/shard_map/ppermute | solution.py:505
  269.3 11.1 %collective-permute-start.23 = (bf16[96,768]{1,0:T(8,128)(2,1)S(1)}, bf16[96,768]{1,0:T(8,128)(2,1)S(1)}, u32[]{:S(2)}, u32[]{:S(2)}) collective-permute-start(bf16[96,768]{1,0:T(8,128)(2,1)S(1)} %add_convert_fusion.4), channel_id=1, source_target_pairs={{0,16},{2,18},{4,20},{6,22},{8,24},{10,26},{12,28},{14,30},{16,0},... | collective-permute-start | bytes 442376 | tf_op jit(solution)/shard_map/ppermute | solution.py:505
  280.5 8.9 %collective-permute-start.24 = (bf16[96,768]{1,0:T(8,128)(2,1)S(1)}, bf16[96,768]{1,0:T(8,128)(2,1)S(1)}, u32[]{:S(2)}, u32[]{:S(2)}) collective-permute-start(bf16[96,768]{1,0:T(8,128)(2,1)S(1)} %add_convert_fusion.3), channel_id=1, source_target_pairs={{0,1},{1,0},{2,3},{3,2},{4,5},{5,4},{6,7},{7,6},{8,9},{9,8},{10,11... | collective-permute-start | bytes 442376 | tf_op jit(solution)/shard_map/ppermute | solution.py:505
  287.0 7.2 %collective-permute-start.12 = (bf16[448,128]{1,0:T(8,128)(2,1)S(1)}, bf16[448,128]{1,0:T(8,128)(2,1)S(1)}, u32[]{:S(2)}, u32[]{:S(2)}) collective-permute-start(bf16[448,128]{1,0:T(8,128)(2,1)S(1)} %maximum_select_fusion.9), channel_id=1, source_target_pairs={{0,1},{1,0},{2,3},{3,2},{4,5},{5,4},{6,7},{7,6},{8,9},{9,8},{10,11... | collective-permute-start | bytes 344072 | tf_op jit(solution)/shard_map/ppermute | solution.py:505
  289.5 18.2 %collective-permute-start.25 = (bf16[192,768]{1,0:T(8,128)(2,1)S(1)}, bf16[192,768]{1,0:T(8,128)(2,1)S(1)}, u32[]{:S(2)}, u32[]{:S(2)}) collective-permute-start(bf16[192,768]{1,0:T(8,128)(2,1)S(1)} %maximum_select_fusion.6), channel_id=1, source_target_pairs={{0,4},{2,6},{4,0},{6,2},{8,12},{10,14},{12,8},{14,10},{16,20},{18,... | collective-permute-start | bytes 884744 | tf_op jit(solution)/shard_map/ppermute | solution.py:505
  292.0 7.1 %collective-permute-start.17 = (bf16[224,128]{1,0:T(8,128)(2,1)S(1)}, bf16[224,128]{1,0:T(8,128)(2,1)S(1)}, u32[]{:S(2)}, u32[]{:S(2)}) collective-permute-start(bf16[224,128]{1,0:T(8,128)(2,1)S(1)} %add_convert_fusion.8), channel_id=1, source_target_pairs={{0,8},{2,10},{4,12},{6,14},{8,0},{10,2},{12,4},{14,6},{16,24},{18,... | collective-permute-start | bytes 172040 | tf_op jit(solution)/shard_map/ppermute | solution.py:505
  294.3 10.3 %collective-permute-start.13 = (bf16[896,128]{1,0:T(8,128)(2,1)S(1)}, bf16[896,128]{1,0:T(8,128)(2,1)S(1)}, u32[]{:S(2)}, u32[]{:S(2)}) collective-permute-start(bf16[896,128]{1,0:T(8,128)(2,1)S(1)} %maximum_select_fusion.7), channel_id=1, source_target_pairs={{0,2},{2,0},{4,6},{6,4},{8,10},{10,8},{12,14},{14,12},{16,18},{18,... | collective-permute-start | bytes 688136 | tf_op jit(solution)/shard_map/ppermute | solution.py:505
  300.8 21.6 %collective-permute-start.28 = (bf16[1,416,384]{2,1,0:T(8,128)(2,1)S(1)}, bf16[1,416,384]{2,1,0:T(8,128)(2,1)S(1)}, u32[]{:S(2)}, u32[]{:S(2)}) collective-permute-start(bf16[1,416,384]{2,1,0:T(8,128)(2,1)S(1)} %add_convert_fusion.1), channel_id=1, source_target_pairs={{0,16},{2,18},{4,20},{6,22},{8,24},{10,26},{12,28},{14,30},{16,0},... | collective-permute-start | bytes 958472 | tf_op jit(solution)/shard_map/ppermute | solution.py:505
  306.7 13.0 %collective-permute-start.20 = (bf16[448,128]{1,0:T(8,128)(2,1)S(1)}, bf16[448,128]{1,0:T(8,128)(2,1)S(1)}, u32[]{:S(2)}, u32[]{:S(2)}) collective-permute-start(bf16[448,128]{1,0:T(8,128)(2,1)S(1)} %maximum_select_fusion.10), channel_id=1, source_target_pairs={{0,1},{1,0},{2,3},{3,2},{4,5},{5,4},{6,7},{7,6},{8,9},{9,8},{10,11... | collective-permute-start | bytes 344072 | tf_op jit(solution)/shard_map/ppermute | solution.py:505
  308.8 27.5 %collective-permute-start.26 = (bf16[384,768]{1,0:T(8,128)(2,1)}, bf16[384,768]{1,0:T(8,128)(2,1)}, u32[]{:S(2)}, u32[]{:S(2)}) collective-permute-start(bf16[384,768]{1,0:T(8,128)(2,1)} %maximum_select_fusion.3), channel_id=1, source_target_pairs={{0,2},{2,0},{4,6},{6,4},{8,10},{10,8},{12,14},{14,12},{16,18},{18,... | collective-permute-start | bytes 1769480 | tf_op jit(solution)/shard_map/ppermute | solution.py:505
  323.2 9.5 %collective-permute-start.29 = (bf16[1,416,384]{2,1,0:T(8,128)(2,1)}, bf16[1,416,384]{2,1,0:T(8,128)(2,1)}, u32[]{:S(2)}, u32[]{:S(2)}) collective-permute-start(bf16[1,416,384]{2,1,0:T(8,128)(2,1)} %add_convert_fusion), channel_id=1, source_target_pairs={{0,4},{2,6},{4,0},{6,2},{8,12},{10,14},{12,8},{14,10},{16,20},{18,... | collective-permute-start | bytes 958472 | tf_op jit(solution)/shard_map/ppermute | solution.py:505
  334.1 5.5 %collective-permute-start.30 = (bf16[2,416,384]{2,1,0:T(8,128)(2,1)S(1)}, bf16[2,416,384]{2,1,0:T(8,128)(2,1)S(1)}, u32[]{:S(2)}, u32[]{:S(2)}) collective-permute-start(bf16[2,416,384]{2,1,0:T(8,128)(2,1)S(1)} %maximum_select_fusion.2), channel_id=1, source_target_pairs={{0,2},{2,0},{4,6},{6,4},{8,10},{10,8},{12,14},{14,12},{16,18},{18,... | collective-permute-start | bytes 1916936 | tf_op jit(solution)/shard_map/ppermute | solution.py:505
  (39 other events, 174.6 us)
Sparse Core Ops, SparseCore 0:
  9.6 24.8 all-gather.6
  36.6 23.9 all-gather.4

commit v3 on v2

--- a/solution.py
+++ b/solution.py
@@ -46,49 +46,92 @@
     return total
 
 
-def attend_kernel(x_ref, seg_ref, wt_ref, bias_ref, xt_ref, qkv_ref, att_ref, lse_ref, qa_ref, ka_ref):
+HB = 1
+LT = 256
+
+
+def attend_kernel(
+    x_ref, seg_ref, w_ref, bias_in_ref, xt_ref, qkv_ref, att_ref, lse_ref,
+    qa_ref, ka_ref, s_ref, p_ref, tot_ref, wt_ref, bias_ref,
+):
     seq, width = x_ref.shape
-    groups = wt_ref.shape[1]
+    groups = wt_ref.shape[0]
     group = width // groups
+
+    @pl.when(pl.program_id(0) == 0)
+    def _():
+        for g in range(groups):
+            for j in range(3):
+                wt_ref[g, j * group : (j + 1) * group, :] = w_ref[j, g].T
+        columns = jnp.concatenate([bias_in_ref[...], jnp.zeros((6, width), F32)], axis=0).T
+        for n in range(2):
+            bias_ref[n] = jnp.broadcast_to(columns[:, n : n + 1], (width, 128))
+
     xt_ref[0] = x_ref[...].T
     seg = seg_ref[0]
     rank = lax.broadcasted_iota(jnp.int32, (16, seq), 0)
     same = rank == seg
-    qa_ref[64:80, :] = jnp.where(same, 1.0, 0.0).astype(BF)
-    ka_ref[64:80, :] = jnp.where(same | (rank >= 4), 0.0, NEG).astype(BF)
-
-    def project(g, carry):
-        rows = pl.ds(pl.multiple_of(g * group, group), group)
-        xg = xt_ref[0, rows, :]
+    for n in range(2 * HB):
+        qa_ref[n, 64:80, :] = jnp.where(same, 1.0, 0.0).astype(BF)
+        ka_ref[n, 64:80, :] = jnp.where(same | (rank >= 4), 0.0, NEG).astype(BF)
+
+    for g in range(groups):
+        rows = slice(g * group, (g + 1) * group)
+        out = dot_nn(wt_ref[g], xt_ref[0, rows, :])
         for j in range(3):
-            out = dot_nn(wt_ref[j, g], xg) + wide(bias_ref[j, rows, :], seq)
-            qkv_ref[0, j, rows, :] = out.astype(BF)
-        return carry
-
-    lax.fori_loop(0, groups, project, 0)
-
-    def head(h, carry):
-        rows = pl.ds(pl.multiple_of(h * HEAD_DIM, HEAD_DIM), HEAD_DIM)
-        qa_ref[0:64, :] = qkv_ref[0, 0, rows, :] * jnp.asarray(0.125, BF)
-        ka_ref[0:64, :] = qkv_ref[0, 1, rows, :]
-        kn = ka_ref[...].T
-        vt = qkv_ref[0, 2, rows, :]
-        for t in range(seq // 256):
-            cols = slice(t * 256, t * 256 + 256)
-            s = dot_nn(kn, qa_ref[:, cols])
-            peak = jnp.max(s, axis=0, keepdims=True)
-            e = jnp.exp(s - peak)
-            total = jnp.sum(e, axis=0, keepdims=True)
-            p = (e * (1.0 / total)).astype(BF)
-            att_ref[0, rows, cols] = dot_nn(vt, p).astype(BF)
-            lse_ref[0, pl.ds(h, 1), cols] = peak + jnp.log(total)
-        return carry
-
-    lax.fori_loop(0, HEADS, head, 0)
-
-
-def attend(x, seg, wt, bias):
+            part = out[j * group : (j + 1) * group]
+            if j != 1:
+                part = part + wide(bias_ref[j // 2, rows, :], seq)
+            qkv_ref[0, j, rows, :] = part.astype(BF)
+
+    def head_rows(h):
+        return slice(h * HEAD_DIM, (h + 1) * HEAD_DIM)
+
+    def scores(h, n):
+        rows = head_rows(h)
+        qa_ref[n, 0:64, :] = qkv_ref[0, 0, rows, :] * jnp.asarray(0.125, BF)
+        ka_ref[n, 0:64, :] = qkv_ref[0, 1, rows, :]
+        s_ref[n] = dot_nn(ka_ref[n].T, qa_ref[n])
+
+    def soften(h, n):
+        for l in range(0, seq, LT):
+            cols = slice(l, l + LT)
+            peak = s_ref[n, 0:8, cols]
+            for c in range(8, seq, 8):
+                peak = jnp.maximum(peak, s_ref[n, c : c + 8, cols])
+            peak = jnp.max(peak, axis=0, keepdims=True)
+            total = jnp.zeros((8, LT), F32)
+            for c in range(0, seq, 16):
+                e = jnp.exp(s_ref[n, c : c + 16, cols] - peak)
+                total = total + (e[0:8] + e[8:16])
+                p_ref[n, c : c + 16, cols] = e.astype(BF)
+            total = jnp.sum(total, axis=0, keepdims=True)
+            tot_ref[n, 0:1, cols] = 1.0 / total
+            tot_ref[n, 1:2, cols] = peak + jnp.log(total)
+        lse_ref[0, h : h + 1, :] = tot_ref[n, 1:2, :]
+
+    def mix(h, n):
+        rows = head_rows(h)
+        att_ref[0, rows, :] = (dot_nn(qkv_ref[0, 2, rows, :], p_ref[n]) * tot_ref[n, 0:1, :]).astype(BF)
+
+    G = HB
+    def many(fn, b):
+        for k in range(G):
+            fn(b * G + k, (b % 2) * G + k)
+
+    batches = HEADS // G
+    for b in range(batches + 2):
+        if b < batches:
+            many(scores, b)
+        if 0 <= b - 1 < batches:
+            many(soften, b - 1)
+        if 0 <= b - 2 < batches:
+            many(mix, b - 2)
+
+
+def attend(x, seg, w, bias):
     width = x.shape[1]
+    groups, group = w.shape[1:3]
     rows, seq = seg.shape
     return pl.pallas_call(
         attend_kernel,
@@ -96,8 +139,8 @@
         in_specs=[
             pl.BlockSpec((seq, width), lambda r: (r, 0)),
             pl.BlockSpec((1, 1, seq), lambda r: (r, 0, 0)),
-            pl.BlockSpec(wt.shape, lambda r: (0, 0, 0, 0)),
-            pl.BlockSpec(bias.shape, lambda r: (0, 0, 0)),
+            pl.BlockSpec(w.shape, lambda r: (0, 0, 0, 0)),
+            pl.BlockSpec(bias.shape, lambda r: (0, 0)),
         ],
         out_specs=[
             pl.BlockSpec((1, width, seq), lambda r: (r, 0, 0)),
@@ -111,27 +154,35 @@
             jax.ShapeDtypeStruct((rows, width, seq), BF),
             jax.ShapeDtypeStruct((rows, 16, seq), F32),
         ],
-        scratch_shapes=[pltpu.VMEM((80, seq), BF), pltpu.VMEM((80, seq), BF)],
+        scratch_shapes=[pltpu.VMEM((2*HB, 80, seq), BF), pltpu.VMEM((2*HB, 80, seq), BF), pltpu.VMEM((2*HB, seq, seq), F32), pltpu.VMEM((2*HB, seq, seq), BF), pltpu.VMEM((2*HB, 8, seq), F32)]
+        + [pltpu.VMEM((groups, 3 * group, group), BF), pltpu.VMEM((2, width, 128), F32)],
         compiler_params=params("arbitrary"),
         name="attend",
-    )(x, seg.reshape(rows, 1, seq), wt, bias)
-
-
-CH = 128
-
-
-def ffn_kernel(
-    xt_ref, att_ref, cot_ref, wot_ref, wo_ref, wu_ref, wut_ref, wd_ref, wdt_ref, vec_ref,
-    out_ref, gr1_ref, gatt_ref, delta_ref, dwo_ref, dff_ref, sums_ref,
+    )(x, seg.reshape(rows, 1, seq), w, bias)
+
+CH = 64
+EC = 64
+DU = 768
+DO = 384
+ROOT_HALF = 0.7071067811865476
+LOG2E = 1.4426950408889634
+
+
+def feed_kernel(
+    core_ref, xt_ref, att_ref, cot_ref, wo_ref, wall_ref, vec_in_ref,
+    out_ref, gr1_ref, gatt_ref, delta_ref, keep_ref, send_ref, okeep_ref, osend_ref,
     a_ref, u1_ref, v2_ref, nlow_ref, act_ref, gp_ref, gd_ref, gup_ref, ct_ref, acc_ref,
+    wot_ref, wut_ref, wdt_ref, vec_ref, dwo_ref, dff_ref,
 ):
     width, seq = a_ref.shape
-    halves, groups = wu_ref.shape[:2]
+    halves, groups = wall_ref.shape[:2]
     group = width // groups
-    part = wut_ref.shape[2]
+    part = wall_ref.shape[3]
+    full = halves * part
     first = pl.program_id(0) == 0
     last = pl.program_id(0) == pl.num_programs(0) - 1
     inv_width = 1.0 / width
+    aug = group + 16
 
     @pl.when(first)
     def _():
@@ -140,73 +191,85 @@
         dff_ref[...] = jnp.zeros_like(dff_ref)
         row = lax.broadcasted_iota(jnp.int32, (16, seq), 0)
         for g in range(groups):
-            nlow_ref[g, group : group + 16, :] = jnp.where(row == 0, 1.0, 0.0).astype(BF)
+            nlow_ref[g, group:aug, :] = jnp.where(row == 0, 1.0, 0.0).astype(BF)
+        columns = vec_in_ref[...].T
+        for n in range(6):
+            vec_ref[n] = jnp.broadcast_to(columns[:, n : n + 1], (width, 128))
+        wot_ref[...] = wo_ref[...].T
+
+        def prepare(i, carry):
+            h, g = i // groups, i % groups
+            rows = pl.ds(pl.multiple_of(h * part, part), part)
+            wut_ref[g, rows, :] = wall_ref[h, g, 0:aug, :].T
+            wdt_ref[g, rows, :] = (wall_ref[h, g, aug : aug + group, :] * jnp.asarray(0.5, BF)).T
+            return carry
+
+        lax.fori_loop(0, halves * groups, prepare, 0)
 
     ct_ref[...] = cot_ref[...].T
 
     part_sum = jnp.zeros((8, seq), F32)
-    for c in range(0, width, CH):
-        s = slice(c, c + CH)
-        v = dot_nn(wot_ref[s, :], att_ref[0]) + wide(vec_ref[0, s, :], seq) + xt_ref[0, s, :].astype(F32)
-        a_ref[s, :] = v
-        part_sum = part_sum + sub_sum(v)
+    for b in range(0, width, DO):
+        mixed = dot_nn(wot_ref[b : b + DO, :], att_ref[0])
+        for c in range(0, DO, EC):
+            s = slice(b + c, b + c + EC)
+            v = mixed[c : c + EC] + wide(vec_ref[0, s, :], seq) + xt_ref[0, s, :].astype(F32)
+            a_ref[s, :] = v
+            part_sum = part_sum + sub_sum(v)
     mean = jnp.sum(part_sum, axis=0, keepdims=True) * inv_width
     part_sum = jnp.zeros((8, seq), F32)
     for c in range(0, width, CH):
-        s = slice(c, c + CH)
-        v = a_ref[s, :] - mean
-        a_ref[s, :] = v
+        v = a_ref[c : c + CH, :] - mean
         part_sum = part_sum + sub_sum(v * v)
     r1 = lax.rsqrt(jnp.sum(part_sum, axis=0, keepdims=True) * inv_width + EPS)
     for g in range(groups):
         for c in range(0, group, 64):
             s = slice(g * group + c, g * group + c + 64)
-            u = a_ref[s, :] * r1
+            u = (a_ref[s, :] - mean) * r1
             u1_ref[s, :] = u
             n = u * wide(vec_ref[1, s, :], seq) + wide(vec_ref[2, s, :], seq)
-            v2_ref[s, :] = n + wide(vec_ref[3, s, :], seq)
+            v2_ref[s, :] = n
             nlow_ref[g, c : c + 64, :] = n.astype(BF)
 
-    def up(i, carry):
-        h, g = i // groups, i % groups
-        for c in range(0, part, CH):
-            s = slice(c, c + CH)
-            u = dot_nn(wut_ref[h, g, s, :], nlow_ref[g])
-            y = u * 0.7071067811865476
-            one = 1.0 + lax.erf(y)
-            act_ref[i, s, :] = (u * one).astype(BF)
-            gp_ref[i, s, :] = one + (y * 1.1283791670955126) * jnp.exp(-(y * y))
-        rows = pl.ds(pl.multiple_of(g * group, group), group)
-        v2_ref[rows, :] += dot_nn(wd_ref[h, g], act_ref[i])
-        return carry
-
-    lax.fori_loop(0, halves * groups, up, 0)
-
     part_sum = jnp.zeros((8, seq), F32)
-    for c in range(0, width, CH):
-        part_sum = part_sum + sub_sum(v2_ref[c : c + CH, :])
+    for g in range(groups):
+        for b in range(0, full, DU):
+            upward = dot_nn(wut_ref[g, b : b + DU, :], nlow_ref[g])
+            for c in range(0, DU, EC):
+                s = slice(b + c, b + c + EC)
+                u = upward[c : c + EC]
+                one = 1.0 + lax.erf(u * ROOT_HALF)
+                act_ref[g, s, :] = (u * one).astype(BF)
+                bell = jnp.exp2((u * u) * (-0.5 * LOG2E))
+                gp_ref[g, s, :] = one + (u * (1.1283791670955126 * ROOT_HALF)) * bell
+        s = slice(g * group, (g + 1) * group)
+        down = dot_nn(wall_ref[0, g, aug : aug + group, :], act_ref[g, 0:part, :])
+        for h in range(1, halves):
+            down = down + dot_nn(wall_ref[h, g, aug : aug + group, :], act_ref[g, h * part : (h + 1) * part, :])
+        v = v2_ref[s, :] + (down * 0.5 + wide(vec_ref[3, s, :], seq))
+        v2_ref[s, :] = v
+        part_sum = part_sum + sub_sum(v)
+
     mean = jnp.sum(part_sum, axis=0, keepdims=True) * inv_width
     part_sum = jnp.zeros((8, seq), F32)
     for c in range(0, width, CH):
-        s = slice(c, c + CH)
-        v = v2_ref[s, :] - mean
-        v2_ref[s, :] = v
+        v = v2_ref[c : c + CH, :] - mean
         part_sum = part_sum + sub_sum(v * v)
     r2 = lax.rsqrt(jnp.sum(part_sum, axis=0, keepdims=True) * inv_width + EPS)
     sum_e = jnp.zeros((8, seq), F32)
     sum_eu = jnp.zeros((8, seq), F32)
     for c in range(0, width, CH):
         s = slice(c, c + CH)
-        u = v2_ref[s, :] * r2
+        u = (v2_ref[s, :] - mean) * r2
         v2_ref[s, :] = u
         gain = wide(vec_ref[4, s, :], seq)
         out_ref[:, s] = (u * gain + wide(vec_ref[5, s, :], seq)).T
         cot = ct_ref[s, :].astype(F32)
-        acc_ref[4, s, :] += fold(cot * u)
+        cu = cot * u
+        acc_ref[4, s, :] += fold(cu)
         acc_ref[5, s, :] += fold(cot)
-        e = cot * gain
-        sum_e = sum_e + sub_sum(e)
-        sum_eu = sum_eu + sub_sum(e * u)
+        sum_e = sum_e + sub_sum(cot * gain)
+        sum_eu = sum_eu + sub_sum(cu * gain)
     mean_e = jnp.sum(sum_e, axis=0, keepdims=True) * inv_width
     mean_eu = jnp.sum(sum_eu, axis=0, keepdims=True) * inv_width
     for c in range(0, width, CH):
@@ -217,30 +280,33 @@
         acc_ref[3, s, :] += fold(gr)
         gd_ref[s, :] = gr.astype(BF)
 
-    def down(i, carry):
-        h, g = i // groups, i % groups
-        rows = pl.ds(pl.multiple_of(g * group, group), group)
-        for c in range(0, part, CH):
-            s = slice(c, c + CH)
-            gup_ref[s, :] = (dot_nn(wdt_ref[h, g, s, :], gd_ref[rows, :]) * gp_ref[i, s, :]).astype(BF)
-        dff_ref[h, g, 0 : group + 16, :] += dot_nt(nlow_ref[g], gup_ref[...])
-        dff_ref[h, g, group + 16 : 2 * group + 16, :] += dot_nt(gd_ref[rows, :], act_ref[i])
-        a_ref[rows, :] += dot_nn(wu_ref[h, g], gup_ref[...])
-        return carry
-
-    lax.fori_loop(0, halves * groups, down, 0)
+    for g in range(groups):
+        rows = slice(g * group, (g + 1) * group)
+        for b in range(0, full, DU):
+            gact = dot_nn(wdt_ref[g, b : b + DU, :], gd_ref[rows, :])
+            for c in range(0, DU, EC):
+                s = slice(b + c, b + c + EC)
+                gup_ref[g % 2, s, :] = (gact[c : c + EC] * gp_ref[g, s, :]).astype(BF)
+        for h in range(halves):
+            s = slice(h * part, (h + 1) * part)
+            dff_ref[h, g, aug : aug + group, :] += dot_nt(gd_ref[rows, :], act_ref[g, s, :])
+            dff_ref[h, g, 0:aug, :] += dot_nt(nlow_ref[g], gup_ref[g % 2, s, :])
+        back = dot_nn(wall_ref[0, g, 0:group, :], gup_ref[g % 2, 0:part, :])
+        for h in range(1, halves):
+            back = back + dot_nn(wall_ref[h, g, 0:group, :], gup_ref[g % 2, h * part : (h + 1) * part, :])
+        a_ref[rows, :] += back
 
     sum_e = jnp.zeros((8, seq), F32)
     sum_eu = jnp.zeros((8, seq), F32)
     for c in range(0, width, CH):
         s = slice(c, c + CH)
         gn = a_ref[s, :]
-        u = u1_ref[s, :]
-        acc_ref[1, s, :] += fold(gn * u)
+        gu = gn * u1_ref[s, :]
+        acc_ref[1, s, :] += fold(gu)
         acc_ref[2, s, :] += fold(gn)
-        e = gn * wide(vec_ref[1, s, :], seq)
-        sum_e = sum_e + sub_sum(e)
-        sum_eu = sum_eu + sub_sum(e * u)
+        gain = wide(vec_ref[1, s, :], seq)
+        sum_e = sum_e + sub_sum(gn * gain)
+        sum_eu = sum_eu + sub_sum(gu * gain)
     mean_e = jnp.sum(sum_e, axis=0, keepdims=True) * inv_width
     mean_eu = jnp.sum(sum_eu, axis=0, keepdims=True) * inv_width
     for c in range(0, width, CH):
@@ -250,46 +316,70 @@
         gr1_ref[0, s, :] = gr
         acc_ref[0, s, :] += fold(gr)
         gd_ref[s, :] = gr.astype(BF)
-    for c in range(0, width, CH):
-        s = slice(c, c + CH)
-        ga = dot_nn(wo_ref[s, :], gd_ref[...]).astype(BF)
-        gatt_ref[0, s, :] = ga
-        prod = ga.astype(F32) * att_ref[0, s, :].astype(F32)
-        for k in range(0, CH, HEAD_DIM):
-            head = (c + k) // HEAD_DIM
-            delta_ref[0, head : head + 1, :] = jnp.sum(prod[k : k + HEAD_DIM], axis=0, keepdims=True)
-        dwo_ref[s, :] += dot_nt(att_ref[0, s, :], gd_ref[...])
+    for b in range(0, width, DO):
+        grad = dot_nn(wo_ref[b : b + DO, :], gd_ref[...])
+        for c in range(0, DO, HEAD_DIM):
+            s = slice(b + c, b + c + HEAD_DIM)
+            ga = grad[c : c + HEAD_DIM].astype(BF)
+            gatt_ref[0, s, :] = ga
+            prod = ga.astype(F32) * att_ref[0, s, :].astype(F32)
+            head = (b + c) // HEAD_DIM
+            delta_ref[0, head : head + 1, :] = jnp.sum(prod, axis=0, keepdims=True)
+    half = width // 2
+    for k in range(2):
+        dwo_ref[k] += dot_nt(att_ref[0, k * half : (k + 1) * half, :], gd_ref[...])
 
     @pl.when(last)
     def _():
-        dff_ref[:, :, group + 16 : 2 * group + 16, :] = dff_ref[:, :, group + 16 : 2 * group + 16, :] * 0.5
         for n in range(6):
-            sums_ref[n : n + 1, :] = jnp.sum(acc_ref[n].T, axis=0, keepdims=True)
-        sums_ref[6:8, :] = jnp.zeros((2, width), F32)
-
-
-def feed(xt, att, cot, wot, wo, wu, wut, wd, wdt, vec):
+            line = jnp.sum(acc_ref[n].T, axis=0, keepdims=True)
+            for k in range(width // part):
+                for h in range(halves):
+                    at = aug + group + n * (width // part) + k
+                    dff_ref[h, 0, at : at + 1, :] = line[:, k * part : (k + 1) * part]
+        core = core_ref[0]
+        okeep_ref[...] = dwo_ref[core]
+        osend_ref[...] = dwo_ref[1 - core].astype(BF)
+        two = groups // 2
+
+        def hand(i, carry):
+            h, k = i // two, i % two
+            for ref, g in ((keep_ref, core * two + k), (send_ref, (1 - core) * two + k)):
+                ref[h, k, 0:aug, :] = dff_ref[h, g, 0:aug, :].astype(ref.dtype)
+                ref[h, k, aug : aug + group, :] = (dff_ref[h, g, aug : aug + group, :] * 0.5).astype(ref.dtype)
+                ref[h, k, aug + group :, :] = dff_ref[h, g, aug + group :, :].astype(ref.dtype)
+            return carry
+
+        lax.fori_loop(0, halves * two, hand, 0)
+
+
+def feed(core, xt, att, cot, wo, wall, vec):
     rows, width, seq = xt.shape
-    halves, groups, group, part = wu.shape
+    halves, groups, depth, part = wall.shape
+    group = width // groups
+    aug = group + 16
+    full = halves * part
 
     def whole(a):
-        return pl.BlockSpec(a.shape, lambda r: (0,) * len(a.shape))
+        return pl.BlockSpec(a.shape, lambda r: (0,) * len(a.shape), pipeline_mode=pl.Buffered(1))
 
     per_row = pl.BlockSpec((1, width, seq), lambda r: (r, 0, 0))
     token = pl.BlockSpec((seq, width), lambda r: (r, 0))
+    sums = (halves, groups // 2, 2 * group + 32, part)
     outs = [
         jax.ShapeDtypeStruct((rows * seq, width), F32),
         jax.ShapeDtypeStruct((rows, width, seq), F32),
         jax.ShapeDtypeStruct((rows, width, seq), BF),
         jax.ShapeDtypeStruct((rows, 16, seq), F32),
-        jax.ShapeDtypeStruct((width, width), F32),
-        jax.ShapeDtypeStruct((halves, groups, 2 * group + 32, part), F32),
-        jax.ShapeDtypeStruct((8, width), F32),
+        jax.ShapeDtypeStruct(sums, F32),
+        jax.ShapeDtypeStruct(sums, BF),
+        jax.ShapeDtypeStruct((width // 2, width), F32),
+        jax.ShapeDtypeStruct((width // 2, width), BF),
     ]
     return pl.pallas_call(
-        ffn_kernel,
+        feed_kernel,
         grid=(rows,),
-        in_specs=[per_row, per_row, token] + [whole(a) for a in (wot, wo, wu, wut, wd, wdt, vec)],
+        in_specs=[pl.BlockSpec(memory_space=pltpu.SMEM), per_row, per_row, token] + [whole(a) for a in (wo, wall, vec)],
         out_specs=[token, per_row, per_row, pl.BlockSpec((1, 16, seq), lambda r: (r, 0, 0))]
         + [whole(a) for a in outs[4:]],
         out_shape=outs,
@@ -297,17 +387,23 @@
             pltpu.VMEM((width, seq), F32),
             pltpu.VMEM((width, seq), F32),
             pltpu.VMEM((width, seq), F32),
-            pltpu.VMEM((groups, group + 16, seq), BF),
-            pltpu.VMEM((halves * groups, part, seq), BF),
-            pltpu.VMEM((halves * groups, part, seq), F32),
+            pltpu.VMEM((groups, aug, seq), BF),
+            pltpu.VMEM((groups, full, seq), BF),
+            pltpu.VMEM((groups, full, seq), F32),
             pltpu.VMEM((width, seq), BF),
-            pltpu.VMEM((part, seq), BF),
+            pltpu.VMEM((2, full, seq), BF),
             pltpu.VMEM((width, seq), BF),
             pltpu.VMEM((6, width, 128), F32),
+            pltpu.VMEM((width, width), BF),
+            pltpu.VMEM((groups, full, aug), BF),
+            pltpu.VMEM((groups, full, group), BF),
+            pltpu.VMEM((6, width, 128), F32),
+            pltpu.VMEM((2, width // 2, width), F32),
+            pltpu.VMEM((halves, groups, 2 * group + 32, part), F32),
         ],
-        compiler_params=params("arbitrary"),
+        compiler_params=pltpu.CompilerParams(vmem_limit_bytes=63 * 2**20),
         name="feed",
-    )(xt, att, cot, wot, wo, wu, wut, wd, wdt, vec)
+    )(core, xt, att, cot, wo, wall, vec)
 
 
 def split3(v):
@@ -551,28 +647,15 @@
     core, ax, rest = bits[0], bits[1], bits[2:]
     ay = Axis("ffn", ffn, 1)
 
-    up_aug = jnp.concatenate(
-        [up_weight, up_bias[:, None, :], jnp.zeros((groups, 15, part), BF)], axis=1
+    wall = jnp.concatenate(
+        [up_weight, up_bias[:, None, :], jnp.zeros((groups, 15, part), BF), down_weight], axis=1
     )
-    up_all = lax.all_gather(up_aug, "ffn", axis=0)
-    down_all = lax.all_gather(down_weight, "ffn", axis=0)
-
-    def lanes(v):
-        return jnp.broadcast_to(v[..., None], v.shape + (128,))
-
-    bias = lanes(jnp.stack([qv_bias[0], jnp.zeros_like(qv_bias[0]), qv_bias[1]]))
-    xt, qkv, att, lse = attend(inputs, segments, qkv_weight.swapaxes(2, 3), bias)
-    vec = lanes(jnp.stack([out_bias, ln1_gain, ln1_bias, down_bias, ln2_gain, ln2_bias]))
-    half = jnp.asarray(0.5, BF)
-    layer_out, gr1, gatt, delta, dwo, dff, sums = feed(
-        xt, att, cotangent, out_weight.T, out_weight,
-        up_all[:, :, :group], up_all.swapaxes(2, 3), down_all * half, down_all.swapaxes(2, 3) * half, vec,
-    )
-    dff = lax.dynamic_update_slice(
-        dff, jnp.broadcast_to(sums[:6].reshape(1, 1, 12, part), (2, 1, 12, part)), (0, 0, 2 * group + 16, 0)
-    )
-
+    wall = lax.all_gather(wall, "ffn", axis=0)
     core_id = core.side.astype(jnp.int32).reshape(1)
+    zero = jnp.zeros_like(out_bias)
+    vec = jnp.stack([out_bias, ln1_gain, ln1_bias, down_bias, ln2_gain, ln2_bias, zero, zero])
+    xt, qkv, att, lse = attend(inputs, segments, qkv_weight, qv_bias)
+    layer_out, gr1, gatt, delta, *first = feed(core_id, xt, att, cotangent, out_weight, wall, vec)
     rows = segments.shape[0]
     step = max(rows // 2, 1)
     parts = 2
@@ -597,8 +680,8 @@
 
     calls = [(index, row0) for index in range(parts) for row0 in range(0, rows, step)]
     calls += [None] * (4 - len(calls))
-    ffn1, out1 = under(calls[0], (core, *core.split(dff.swapaxes(0, 1))), (core, *core.split(dwo)))
-    ffn2, out2 = under(calls[1], (ay, *ay.split(ffn1.swapaxes(0, 1))), (ax, *ax.split(out1)))
+    ffn1, out1 = under(calls[0], (core, *first[:2]), (core, *first[2:]))
+    ffn2, out2 = under(calls[1], (ay, *ay.split(ffn1)), (ax, *ax.split(out1)))
     ffn3, out3, sum0 = under(calls[2], (ax, *ax.split(ffn2[0])), (ay, *ay.split(out2)), (core, *packs[0]))
     low, olow = ffn3.astype(BF), out3.astype(BF)
     ffn4, out4, sum0 = under(
@@ -609,8 +692,8 @@
     grad_inputs = state["grad_inputs"]
     totals = [gather_up(sum_across(sum_down(sum0, [ax]), rest), [core, ay, ax])]
     pkeep, psend = packs[1]
-    first = add(pkeep, core.swap(psend))
-    totals.append(gather_up(sum_across(sum_down(first, [ay, ax]), rest), [core, ay, ax]))
+    last = add(pkeep, core.swap(psend))
+    totals.append(gather_up(sum_across(sum_down(last, [ay, ax]), rest), [core, ay, ax]))
     grads, biases = [], []
     for total in totals:
         total = total.astype(F32)
@@ -652,15 +735,3 @@
         out_specs=(rows, rows) + (shared,) * 6 + (split, P(None, "ffn"), split) + (shared,) * 3,
         check_vma=False,
     )
-
-
-def specs(which):
-    bf, f, i = jnp.bfloat16, jnp.float32, jnp.int32
-    if which == "attend":
-        return attend, [((2048, 768), bf), ((4, 512), i), ((3, 4, 192, 192), bf), ((3, 768, 128), f)]
-    if which == "feed":
-        return feed, [((4, 768, 512), bf), ((4, 768, 512), bf), ((2048, 768), bf), ((768, 768), bf), ((768, 768), bf), ((2, 4, 192, 384), bf),
-                      ((2, 4, 384, 208), bf), ((2, 4, 192, 384), bf), ((2, 4, 384, 192), bf), ((6, 768, 128), f)]
-    if which == "back":
-        return (lambda *a: back(*a, 0, 2, None)), [((4, 3, 768, 512), bf), ((4, 768, 512), bf), ((4, 768, 512), bf), ((4, 768, 512), f),
-                                                   ((4, 16, 512), f), ((4, 16, 512), f), ((4, 512), i), ((3, 4, 192, 192), bf)]

time: 353 us -> 280 us (0.79)
  Pallas kernels: 209 us -> 145 us
  waiting for transfers between devices: 22 us -> 42 us
  local copies, waits for them, and re-layouts: 38.5 us -> 19 us
  starting transfers between devices: 46.6 us -> 39.4 us
    pallas_call x1, Pallas kernels: 63 us -> 22.4 us  [attend(): pl.pallas_call(attend_kernel, grid=(rows,), in_specs=[pl.BlockSpec((seq,...]
    pallas_call x1, Pallas kernels: 82.3 us -> 58.3 us  [feed(): pl.pallas_call(feed_kernel, grid=(rows,), in_specs=[pl.BlockSpec(memory_s...]
    all_gather x2 -> x1, waiting for transfers between devices: 0.02 us -> 15.6 us  [per_device(): wall = lax.all_gather(wall, 'ffn', axis=0)]
    ppermute x31, starting transfers between devices: 46.6 us -> 39.4 us  [swap(): return lax.ppermute(value, self.name, self.pairs)]
    ppermute x31, waiting for transfers between devices: 21.2 us -> 26.4 us  [swap(): return lax.ppermute(value, self.name, self.pairs)]
    broadcast_in_dim x4 -> x0, local copies, waits for them, and re-layouts: 3.91 us -> none  [the longest x2 3.16 us: lanes(): return jnp.broadcast_to(v[..., None], v.shape + (128,))]
    unnamed x66 -> x48, local copies, waits for them, and re-layouts: 8.3 us -> 4.57 us
    dynamic_slice x8 -> x5, local copies, waits for them, and re-layouts: 7.29 us -> 4.35 us  [split(): keep = lax.dynamic_slice_in_dim(value, self.side * half, half, 0)]
  transfers between devices with their start and end apart: 33 -> 32, of which waited for: 9 -> 9; matrix products, arithmetic and copies ran while one was open for 11% -> 10% of each run, Pallas kernels for 36% -> 31%
where the time goes in v3:
time: 280 us
  Pallas kernels  145 us (52%)
  waiting for transfers between devices  42 us (15%)
  starting transfers between devices  39.4 us (14%)
  other arithmetic  20.3 us (7%)
  local copies, waits for them, and re-layouts  19 us (7%)
  between operations  14.6 us (5%)
    pallas_call x4, Pallas kernels, back(): pl.pallas_call(partial(back_kernel, head0=index * (chans // HEAD_DIM), fr...  63.8 us
    pallas_call x1, Pallas kernels, feed(): pl.pallas_call(feed_kernel, grid=(rows,), in_specs=[pl.BlockSpec(memory_s...  58.3 us
    ppermute x31, starting transfers between devices, swap(): return lax.ppermute(value, self.name, self.pairs)  39.4 us
    ppermute x31, waiting for transfers between devices, swap(): return lax.ppermute(value, self.name, self.pairs)  26.4 us
    pallas_call x1, Pallas kernels, attend(): pl.pallas_call(attend_kernel, grid=(rows,), in_specs=[pl.BlockSpec((seq,...  22.4 us
    all_gather x1, waiting for transfers between devices, per_device(): wall = lax.all_gather(wall, 'ffn', axis=0)  15.6 us
  transfers between devices with their start and end apart: 32, of which 9 were waited for; matrix products, arithmetic and copies ran while one was open for 10% of the time, Pallas kernels for 31%

profile of v3, /device:TPU:1, one launch (start us, length us, event | category | flops | bytes accessed | tf_op | source)
XLA Modules:
  0.0 280.0 jit_solution(3992096623712037511)
XLA Ops:
  8.0 2.6 pad_maximum_fusion.1
  11.4 22.4 %attend.1 = (bf16[4,768,512]{2,1,0:T(8,128)(2,1)}, bf16[4,3,768,512]{3,2,1,0:T(8,128)(2,1)}, bf16[4,768,512]{2,1,0:T(8,128)(2,1)}, f32[4,16,512]{2,1,0:T(8,128)}) custom-call(bf16[2048,768]{1,0:T(8,128)(2,1)} %x_ref.1, s32[4,1,512]{2,1,0:T(1,128)} %reshape.90.seg_ref, bf16[3,4,192,192]{3,2,1,0:T(8,128)(2,1)} %w_ref.9, f32[2,768]{1,0:T(2,128)} %bias_in_ref.1), custom_call_target="tpu_custom_call" | custom-call | tf_op jit(solution)/shard_map/attend/pallas_call | solution.py:136
  34.5 15.6 %all-gather.3.cloned.1.call-done = bf16[8,400,384]{2,1,0:T(8,128)(2,1)} async-done(((bf16[4,400,384]{2,1,0:T(8,128)(2,1)}), bf16[8,400,384]{2,1,0:T(8,128)(2,1)}) %all-gather.3.cloned.1.call-update) | async-done | bytes 2457616 | tf_op jit(solution)/shard_map/all_gather | solution.py:653
  50.1 58.3 %feed.1 = (f32[2048,768]{1,0:T(8,128)}, f32[4,768,512]{2,1,0:T(8,128)}, bf16[4,768,512]{2,1,0:T(8,128)(2,1)}, f32[4,16,512]{2,1,0:T(8,128)}, f32[2,2,416,384]{3,...) custom-call(s32[1]{0:T(128)} %bitcast.core_ref, ...), custom_call_target="tpu_custom_call" | custom-call | tf_op jit(solution)/shard_map/feed/pallas_call | solution.py:379
  109.4 15.6 %back.4 = (f32[2,2,416,384]{3,2,1,0:T(8,128)}, f32[384,768]{1,0:T(8,128)}, f32[2048,768]{1,0:T(8,128)}, f32[3,2,192,192]{3,2,1,0:T(8,128)}, f32[2,384,128]{2,1,0:T(8,128)}) custom-call(s32[1]{0:T(128)} %bitcast.core_ref, bf16[4,3,768,512]{3,2,1,0:T(8,128)(2,1)} %get-tuple-element.51.qkv_ref, ...), custom_call_target="tpu_custom_call", output_to_operand_aliasing={{0}: (9, {}), {1}: (10, {})} | custom-call | flops 7000000000 | bytes 20971520 | tf_op jit(solution)/shard_map/back/pallas_call | solution.py:574
  131.0 16.3 %back.5 = (f32[1,2,416,384]{3,2,1,0:T(8,128)}, f32[192,768]{1,0:T(8,128)}, f32[2048,768]{1,0:T(8,128)}, f32[896,128]{1,0:T(8,128)}, bf16[896,128]{1,0:T(8,128)(2,1)}) custom-call(s32[1]{0:T(128)} %bitcast.core_ref, bf16[4,3,768,512]{3,2,1,0:T(8,128)(2,1)} %get-tuple-element.51.qkv_ref, ...), custom_call_target="tpu_custom_call", output_to_operand_aliasing={{2}: (11, {}), {0}: (12, {}), {1}: (13, {})} | custom-call | flops 7000000000 | bytes 20971520 | tf_op jit(solution)/shard_map/back/pallas_call | solution.py:574
  153.2 15.5 %back.6 = (f32[1,416,384]{2,1,0:T(8,128)}, f32[96,768]{1,0:T(8,128)}, f32[896,128]{1,0:T(8,128)}, f32[2048,768]{1,0:T(8,128)}, f32[3,2,192,192]{3,2,1,0:T(8,128)}, /*index=5*/f32[2,384,128]{2,1,0:T(8,128)}) custom-call(s32[1]{0:T(128)} %bitcast.core_ref, ...), custom_call_target="tpu_custom_call", output_to_operand_aliasing={{3}: (9, {}), {0}: (10, {}), {1}: (11, {}), {2}: (12, {})} | custom-call | flops 7000000000 | bytes 20971520 | tf_op jit(solution)/shard_map/back/pallas_call | solution.py:574
  173.1 16.4 %back.7 = (f32[1,416,384]{2,1,0:T(8,128)}, f32[96,768]{1,0:T(8,128)}, f32[448,128]{1,0:T(8,128)}, f32[2048,768]{1,0:T(8,128)}, f32[896,128]{1,0:T(8,128)}, /*index=5*/bf16[896,128]{1,0:T(8,128)(2,1)}) custom-call(s32[1]{0:T(128)} %bitcast.core_ref, ...), custom_call_target="tpu_custom_call", output_to_operand_aliasing={{3}: (11, {}), {0}: (12, {}), {1}: (13, {}), {2}: (14, {})} | custom-call | flops 7000000000 | bytes 20971520 | tf_op jit(solution)/shard_map/back/pallas_call | solution.py:574
  197.0 2.2 collective-permute-start.23
  199.2 8.0 %collective-permute-done.9 = bf16[224,128]{1,0:T(8,128)(2,1)S(1)} collective-permute-done((bf16[224,128]{1,0:T(8,128)(2,1)S(1)}, bf16[224,128]{1,0:T(8,128)(2,1)S(1)}, u32[]{:S(2)}, u32[]{:S(2)}) %collective-permute-start.9) | collective-permute-done | bytes 57376 | tf_op jit(solution)/shard_map/ppermute | solution.py:601
  208.9 2.9 %collective-permute-done.10 = bf16[224,128]{1,0:T(8,128)(2,1)S(1)} collective-permute-done((bf16[224,128]{1,0:T(8,128)(2,1)S(1)}, bf16[224,128]{1,0:T(8,128)(2,1)S(1)}, u32[]{:S(2)}, u32[]{:S(2)}) %collective-permute-start.10) | collective-permute-done | bytes 57376 | tf_op jit(solution)/shard_map/ppermute | solution.py:601
  213.5 1.7 collective-permute-done.11
  218.0 1.7 collective-permute-done.16
  219.7 2.0 collective-permute-start.17
  221.8 4.8 %collective-permute-start.13 = (bf16[896,128]{1,0:T(8,128)(2,1)S(1)}, bf16[896,128]{1,0:T(8,128)(2,1)S(1)}, u32[]{:S(2)}, u32[]{:S(2)}) collective-permute-start(bf16[896,128]{1,0:T(8,128)(2,1)S(1)} %maximum_select_fusion.7), channel_id=1, source_target_pairs={{0,2},{2,0},{4,6},{6,4},{8,10},{10,8},{12,14},{14,12},{16,18},{18,... | collective-permute-start | bytes 688136 | tf_op jit(solution)/shard_map/ppermute | solution.py:601
  226.7 1.7 collective-permute-start.18
  229.2 6.1 %collective-permute-done.18 = bf16[224,128]{1,0:T(8,128)(2,1)S(1)} collective-permute-done((bf16[224,128]{1,0:T(8,128)(2,1)S(1)}, bf16[224,128]{1,0:T(8,128)(2,1)S(1)}, u32[]{:S(2)}, u32[]{:S(2)}) %collective-permute-start.18) | collective-permute-done | bytes 57376 | tf_op jit(solution)/shard_map/ppermute | solution.py:601
  235.6 3.1 %collective-permute-done.19 = bf16[224,128]{1,0:T(8,128)(2,1)S(1)} collective-permute-done((bf16[224,128]{1,0:T(8,128)(2,1)S(1)}, bf16[224,128]{1,0:T(8,128)(2,1)S(1)}, u32[]{:S(2)}, u32[]{:S(2)}) %collective-permute-start.19) | collective-permute-done | bytes 57376 | tf_op jit(solution)/shard_map/ppermute | solution.py:601
  241.2 6.5 %collective-permute-start.26 = (bf16[384,768]{1,0:T(8,128)(2,1)}, bf16[384,768]{1,0:T(8,128)(2,1)}, u32[]{:S(2)}, u32[]{:S(2)}) collective-permute-start(bf16[384,768]{1,0:T(8,128)(2,1)} %maximum_select_fusion.3), channel_id=1, source_target_pairs={{0,2},{2,0},{4,6},{6,4},{8,10},{10,8},{12,14},{14,12},{16,18},{18,... | collective-permute-start | bytes 1769480 | tf_op jit(solution)/shard_map/ppermute | solution.py:601
  247.8 2.1 collective-permute-start.21
  255.6 2.1 copy.55
  257.7 2.5 collective-permute-done.29
  263.8 3.3 %fusion.1 = f32[768,768]{1,0:T(8,128)} fusion(bf16[384,768]{1,0:T(8,128)(2,1)} %collective-permute-done.26, bf16[384,768]{1,0:T(8,128)(2,1)} %maximum_select_fusion.3, pred[]{:T(512)S(6)} %eq.10), kind=kLoop, calls=%fused_computation.8 | loop fusion | flops 5898240 | bytes 3538945 | tf_op jit(solution)/shard_map/convert_element_type | solution.py:691
  267.4 1.6 fusion.8
  (172 shorter events, 50.1 us)
Async XLA Ops:
  7.2 42.9 %all-gather.3.cloned.1.call-start = ((), (), s32[]{:S(2)}) async-start(), calls=%async_computation | async-start | bytes 3686400 | tf_op jit(solution)/shard_map/all_gather | solution.py:653
  108.4 20.2 %collective-permute-start = (bf16[2,2,416,384]{3,2,1,0:T(8,128)(2,1)}, bf16[2,2,416,384]{3,2,1,0:T(8,128)(2,1)S(1)}, u32[]{:S(2)}, u32[]{:S(2)}) collective-permute-start(bf16[2,2,416,384]{3,2,1,0:T(8,128)(2,1)} %get-tuple-element.58.rest_2_), channel_id=1, source_target_pairs={{0,2},{2,0},{4,6},{6,4},{8,10},{10,8},{12,14},{14,12},{16,18},{18,... | collective-permute-start | bytes 3833864 | tf_op jit(solution)/shard_map/ppermute | solution.py:601
  109.2 15.8 %collective-permute-start.1 = (bf16[384,768]{1,0:T(8,128)(2,1)}, bf16[384,768]{1,0:T(8,128)(2,1)S(1)}, u32[]{:S(2)}, u32[]{:S(2)}) collective-permute-start(bf16[384,768]{1,0:T(8,128)(2,1)} %get-tuple-element.59.rest_3_), channel_id=1, source_target_pairs={{0,2},{2,0},{4,6},{6,4},{8,10},{10,8},{12,14},{14,12},{16,18},{18,... | collective-permute-start | bytes 1769480 | tf_op jit(solution)/shard_map/ppermute | solution.py:601
  126.6 20.8 %collective-permute-start.3 = (bf16[192,768]{1,0:T(8,128)(2,1)S(1)}, bf16[192,768]{1,0:T(8,128)(2,1)S(1)}, u32[]{:S(2)}, u32[]{:S(2)}) collective-permute-start(bf16[192,768]{1,0:T(8,128)(2,1)S(1)} %dynamic-slice_convert_fusion.2.rest_6_), channel_id=1, source_target_pairs={{0,4},{2,6},{4,0},{6,2},{8,12},{10,14},{12,8},{14,10},{16,20},{18,... | collective-permute-start | bytes 884744 | tf_op jit(solution)/shard_map/ppermute | solution.py:601
  130.2 21.2 %collective-permute-start.2 = (bf16[1,2,416,384]{3,2,1,0:T(8,128)(2,1)S(1)}, bf16[1,2,416,384]{3,2,1,0:T(8,128)(2,1)S(1)}, u32[]{:S(2)}, u32[]{:S(2)}) collective-permute-start(bf16[1,2,416,384]{3,2,1,0:T(8,128)(2,1)S(1)} %dynamic-slice_convert_fusion.rest_5_), channel_id=1, source_target_pairs={{0,1},{1,0},{2,3},{3,2},{4,5},{5,4},{6,7},{7,6},{8,9},{9,8},{10,11... | collective-permute-start | bytes 1916936 | tf_op jit(solution)/shard_map/ppermute | solution.py:601
  148.7 22.5 %collective-permute-start.5 = (bf16[96,768]{1,0:T(8,128)(2,1)S(1)}, bf16[96,768]{1,0:T(8,128)(2,1)S(1)}, u32[]{:S(2)}, u32[]{:S(2)}) collective-permute-start(bf16[96,768]{1,0:T(8,128)(2,1)S(1)} %dynamic-slice_convert_fusion.3.rest_5_), channel_id=1, source_target_pairs={{0,1},{1,0},{2,3},{3,2},{4,5},{5,4},{6,7},{7,6},{8,9},{9,8},{10,11... | collective-permute-start | bytes 442376 | tf_op jit(solution)/shard_map/ppermute | solution.py:601
  149.5 19.3 %collective-permute-start.6 = (bf16[896,128]{1,0:T(8,128)(2,1)S(1)}, bf16[896,128]{1,0:T(8,128)(2,1)S(1)}, u32[]{:S(2)}, u32[]{:S(2)}) collective-permute-start(bf16[896,128]{1,0:T(8,128)(2,1)S(1)} %copy-done.14), channel_id=1, source_target_pairs={{0,2},{2,0},{4,6},{6,4},{8,10},{10,8},{12,14},{14,12},{16,18},{18,... | collective-permute-start | bytes 688136 | tf_op jit(solution)/shard_map/ppermute | solution.py:601
  152.5 19.5 %collective-permute-start.4 = (bf16[1,416,384]{2,1,0:T(8,128)(2,1)S(1)}, bf16[1,416,384]{2,1,0:T(8,128)(2,1)S(1)}, u32[]{:S(2)}, u32[]{:S(2)}) collective-permute-start(bf16[1,416,384]{2,1,0:T(8,128)(2,1)S(1)} %fusion.4.rest_4_), channel_id=1, source_target_pairs={{0,4},{2,6},{4,0},{6,2},{8,12},{10,14},{12,8},{14,10},{16,20},{18,... | collective-permute-start | bytes 958472 | tf_op jit(solution)/shard_map/ppermute | solution.py:601
  170.0 19.5 %collective-permute-start.7 = (bf16[448,128]{1,0:T(8,128)(2,1)S(1)}, bf16[448,128]{1,0:T(8,128)(2,1)S(1)}, u32[]{:S(2)}, u32[]{:S(2)}) collective-permute-start(bf16[448,128]{1,0:T(8,128)(2,1)S(1)} %dynamic-slice_convert_fusion.5.rest_8_), channel_id=1, source_target_pairs={{0,1},{1,0},{2,3},{3,2},{4,5},{5,4},{6,7},{7,6},{8,9},{9,8},{10,11... | collective-permute-start | bytes 344072 | tf_op jit(solution)/shard_map/ppermute | solution.py:601
  192.7 35.6 %collective-permute-start.27 = (bf16[1,416,384]{2,1,0:T(8,128)(2,1)S(1)}, bf16[1,416,384]{2,1,0:T(8,128)(2,1)S(1)}, u32[]{:S(2)}, u32[]{:S(2)}) collective-permute-start(bf16[1,416,384]{2,1,0:T(8,128)(2,1)S(1)} %copy-done.7), channel_id=1, source_target_pairs={{0,8},{2,10},{4,12},{6,14},{8,0},{10,2},{12,4},{14,6},{16,24},{18,... | collective-permute-start | bytes 958472 | tf_op jit(solution)/shard_map/ppermute | solution.py:601
  192.9 19.3 %collective-permute-start.14 = (bf16[896,128]{1,0:T(8,128)(2,1)}, bf16[896,128]{1,0:T(8,128)(2,1)S(1)}, u32[]{:S(2)}, u32[]{:S(2)}) collective-permute-start(bf16[896,128]{1,0:T(8,128)(2,1)} %get-tuple-element.79), channel_id=1, source_target_pairs={{0,2},{2,0},{4,6},{6,4},{8,10},{10,8},{12,14},{14,12},{16,18},{18,... | collective-permute-start | bytes 688136 | tf_op jit(solution)/shard_map/ppermute | solution.py:601
  194.4 12.9 %collective-permute-start.9 = (bf16[224,128]{1,0:T(8,128)(2,1)S(1)}, bf16[224,128]{1,0:T(8,128)(2,1)S(1)}, u32[]{:S(2)}, u32[]{:S(2)}) collective-permute-start(bf16[224,128]{1,0:T(8,128)(2,1)S(1)} %add_convert_fusion.11), channel_id=1, source_target_pairs={{0,8},{2,10},{4,12},{6,14},{8,0},{10,2},{12,4},{14,6},{16,24},{18,... | collective-permute-start | bytes 172040 | tf_op jit(solution)/shard_map/ppermute | solution.py:601
  197.0 10.9 %collective-permute-start.23 = (bf16[96,768]{1,0:T(8,128)(2,1)S(1)}, bf16[96,768]{1,0:T(8,128)(2,1)S(1)}, u32[]{:S(2)}, u32[]{:S(2)}) collective-permute-start(bf16[96,768]{1,0:T(8,128)(2,1)S(1)} %add_convert_fusion.4), channel_id=1, source_target_pairs={{0,16},{2,18},{4,20},{6,22},{8,24},{10,26},{12,28},{14,30},{16,0},... | collective-permute-start | bytes 442376 | tf_op jit(solution)/shard_map/ppermute | solution.py:601
  207.9 9.5 %collective-permute-start.24 = (bf16[96,768]{1,0:T(8,128)(2,1)S(1)}, bf16[96,768]{1,0:T(8,128)(2,1)S(1)}, u32[]{:S(2)}, u32[]{:S(2)}) collective-permute-start(bf16[96,768]{1,0:T(8,128)(2,1)S(1)} %add_convert_fusion.3), channel_id=1, source_target_pairs={{0,1},{1,0},{2,3},{3,2},{4,5},{5,4},{6,7},{7,6},{8,9},{9,8},{10,11... | collective-permute-start | bytes 442376 | tf_op jit(solution)/shard_map/ppermute | solution.py:601
  215.2 6.6 %collective-permute-start.12 = (bf16[448,128]{1,0:T(8,128)(2,1)S(1)}, bf16[448,128]{1,0:T(8,128)(2,1)S(1)}, u32[]{:S(2)}, u32[]{:S(2)}) collective-permute-start(bf16[448,128]{1,0:T(8,128)(2,1)S(1)} %maximum_select_fusion.9), channel_id=1, source_target_pairs={{0,1},{1,0},{2,3},{3,2},{4,5},{5,4},{6,7},{7,6},{8,9},{9,8},{10,11... | collective-permute-start | bytes 344072 | tf_op jit(solution)/shard_map/ppermute | solution.py:601
  217.4 22.8 %collective-permute-start.25 = (bf16[192,768]{1,0:T(8,128)(2,1)S(1)}, bf16[192,768]{1,0:T(8,128)(2,1)S(1)}, u32[]{:S(2)}, u32[]{:S(2)}) collective-permute-start(bf16[192,768]{1,0:T(8,128)(2,1)S(1)} %maximum_select_fusion.6), channel_id=1, source_target_pairs={{0,4},{2,6},{4,0},{6,2},{8,12},{10,14},{12,8},{14,10},{16,20},{18,... | collective-permute-start | bytes 884744 | tf_op jit(solution)/shard_map/ppermute | solution.py:601
  219.7 6.9 %collective-permute-start.17 = (bf16[224,128]{1,0:T(8,128)(2,1)S(1)}, bf16[224,128]{1,0:T(8,128)(2,1)S(1)}, u32[]{:S(2)}, u32[]{:S(2)}) collective-permute-start(bf16[224,128]{1,0:T(8,128)(2,1)S(1)} %add_convert_fusion.8), channel_id=1, source_target_pairs={{0,8},{2,10},{4,12},{6,14},{8,0},{10,2},{12,4},{14,6},{16,24},{18,... | collective-permute-start | bytes 172040 | tf_op jit(solution)/shard_map/ppermute | solution.py:601
  221.8 13.6 %collective-permute-start.13 = (bf16[896,128]{1,0:T(8,128)(2,1)S(1)}, bf16[896,128]{1,0:T(8,128)(2,1)S(1)}, u32[]{:S(2)}, u32[]{:S(2)}) collective-permute-start(bf16[896,128]{1,0:T(8,128)(2,1)S(1)} %maximum_select_fusion.7), channel_id=1, source_target_pairs={{0,2},{2,0},{4,6},{6,4},{8,10},{10,8},{12,14},{14,12},{16,18},{18,... | collective-permute-start | bytes 688136 | tf_op jit(solution)/shard_map/ppermute | solution.py:601
  226.7 8.6 %collective-permute-start.18 = (bf16[224,128]{1,0:T(8,128)(2,1)S(1)}, bf16[224,128]{1,0:T(8,128)(2,1)S(1)}, u32[]{:S(2)}, u32[]{:S(2)}) collective-permute-start(bf16[224,128]{1,0:T(8,128)(2,1)S(1)} %add_convert_fusion.7), channel_id=1, source_target_pairs={{0,16},{2,18},{4,20},{6,22},{8,24},{10,26},{12,28},{14,30},{16,0},... | collective-permute-start | bytes 172040 | tf_op jit(solution)/shard_map/ppermute | solution.py:601
  228.4 21.6 %collective-permute-start.28 = (bf16[1,416,384]{2,1,0:T(8,128)(2,1)S(1)}, bf16[1,416,384]{2,1,0:T(8,128)(2,1)S(1)}, u32[]{:S(2)}, u32[]{:S(2)}) collective-permute-start(bf16[1,416,384]{2,1,0:T(8,128)(2,1)S(1)} %add_convert_fusion.1), channel_id=1, source_target_pairs={{0,16},{2,18},{4,20},{6,22},{8,24},{10,26},{12,28},{14,30},{16,0},... | collective-permute-start | bytes 958472 | tf_op jit(solution)/shard_map/ppermute | solution.py:601
  238.8 9.0 %collective-permute-start.20 = (bf16[448,128]{1,0:T(8,128)(2,1)S(1)}, bf16[448,128]{1,0:T(8,128)(2,1)S(1)}, u32[]{:S(2)}, u32[]{:S(2)}) collective-permute-start(bf16[448,128]{1,0:T(8,128)(2,1)S(1)} %maximum_select_fusion.10), channel_id=1, source_target_pairs={{0,1},{1,0},{2,3},{3,2},{4,5},{5,4},{6,7},{7,6},{8,9},{9,8},{10,11... | collective-permute-start | bytes 344072 | tf_op jit(solution)/shard_map/ppermute | solution.py:601
  241.2 22.6 %collective-permute-start.26 = (bf16[384,768]{1,0:T(8,128)(2,1)}, bf16[384,768]{1,0:T(8,128)(2,1)}, u32[]{:S(2)}, u32[]{:S(2)}) collective-permute-start(bf16[384,768]{1,0:T(8,128)(2,1)} %maximum_select_fusion.3), channel_id=1, source_target_pairs={{0,2},{2,0},{4,6},{6,4},{8,10},{10,8},{12,14},{14,12},{16,18},{18,... | collective-permute-start | bytes 1769480 | tf_op jit(solution)/shard_map/ppermute | solution.py:601
  250.8 9.5 %collective-permute-start.29 = (bf16[1,416,384]{2,1,0:T(8,128)(2,1)}, bf16[1,416,384]{2,1,0:T(8,128)(2,1)}, u32[]{:S(2)}, u32[]{:S(2)}) collective-permute-start(bf16[1,416,384]{2,1,0:T(8,128)(2,1)} %add_convert_fusion), channel_id=1, source_target_pairs={{0,4},{2,6},{4,0},{6,2},{8,12},{10,14},{12,8},{14,10},{16,20},{18,... | collective-permute-start | bytes 958472 | tf_op jit(solution)/shard_map/ppermute | solution.py:601
  261.6 5.5 %collective-permute-start.30 = (bf16[2,416,384]{2,1,0:T(8,128)(2,1)S(1)}, bf16[2,416,384]{2,1,0:T(8,128)(2,1)S(1)}, u32[]{:S(2)}, u32[]{:S(2)}) collective-permute-start(bf16[2,416,384]{2,1,0:T(8,128)(2,1)S(1)} %maximum_select_fusion.2), channel_id=1, source_target_pairs={{0,2},{2,0},{4,6},{6,4},{8,10},{10,8},{12,14},{14,12},{16,18},{18,... | collective-permute-start | bytes 1916936 | tf_op jit(solution)/shard_map/ppermute | solution.py:601
  (30 other events, 156.7 us)
Sparse Core Ops, SparseCore 0:
  10.8 39.2 all-gather.2
